TPU v7x, 512 devices: a whole 4x8x8 slice. The times are simulated.
512 devices in a mesh: grp: 16 (over z, core), hap: 32 (over x, y).
Axes of the slice: x: 4, y: 8, z: 8, core: 2. Of those that a mesh axis runs over, the one named last changes fastest.
Arguments:
- alleles: int32 [240, 512], P('grp', 'hap'), may hold values from 0 to 1073741823
- observed: int32 [240, 128], P('grp', 'hap'), may hold values from 0 to 2
- map_steps: int32 [240], P('grp'), may hold values from 1 to 99
- start_weights: float32 [128, 15360], P('hap'), may hold values from 1e-12 to 1
- end_weights: float32 [128, 15360], P('hap'), may hold values from 1e-12 to 1
Outputs:
- dosage: float32 [240, 128], P('grp', 'hap')
Inputs may be any that keep to these rules, and one draw needn't show every extreme that they name: Bit b of alleles[m, w] is the allele 0 or 1 of reference haplotype 30 w + b at marker m. 0 and 1 are observed alleles, 2 marks a marker not typed in that target.
All inputs are finite; a program needn't handle non-finite values.
Results may differ from a plain program's by a relative error of at most 0.0008.
Values sent between devices are 32-bit elements; how exact they have to be, the bound alone decides.
No kernel may reach another device: no remote copies, remote signals or barrier semaphores. Data moves between devices by JAX's collectives and lax.ppermute only.
A program may use at most 128 MiB of HBM per device.

v0:
```python
import jax
import jax.numpy as jnp
from jax import lax
from jax.sharding import PartitionSpec as P

error_rate = 0.01
map_unit = 100000.0


def joined_along(tiles, dim):
    lengths = list(tiles.shape[1:])
    lengths[dim] *= tiles.shape[0]
    return jnp.moveaxis(tiles, 0, dim).reshape(lengths)


def sent_to_all(array, axis):
    peers = lax.axis_size(axis)
    return lax.all_to_all(
        jnp.broadcast_to(array[None], (peers, *array.shape)), axis, 0, 0, tiled=True
    )


def gather_directly(array, axis, dim):
    return joined_along(sent_to_all(array, axis), dim)


def passed_along(value, axis, steps):
    count = lax.axis_size(axis)
    initial, last = (max(0, -steps), min(count, count - steps))
    return lax.ppermute(value, axis, [(source, source + steps) for source in range(initial, last)])


def unpack_alleles(packed):
    shifts = jnp.arange(30, dtype=jnp.int32)
    bits = jnp.bitwise_and(jnp.right_shift(packed[:, :, None], shifts[None, None, :]), 1)
    return bits.reshape(packed.shape[0], packed.shape[1] * 30).astype(jnp.float32)


def emission(allele_row, observed_col):
    missing = (observed_col == 2).astype(jnp.float32)[:, None]
    called = observed_col.astype(jnp.float32)[:, None]
    agree = allele_row[None, :] * called + (1.0 - allele_row[None, :]) * (1.0 - called)
    return missing + (1.0 - missing) * (error_rate + (1.0 - 2.0 * error_rate) * agree)


def forward_pass(state, haplos, observed, rates):
    total_haps = haplos.shape[1]

    def advance(carry, inputs):
        allele_row, observed_col, rate = inputs
        mixed = (1.0 - rate) * carry + rate / total_haps * jnp.sum(carry, axis=1, keepdims=True)
        weighted = emission(allele_row, observed_col) * mixed
        weighted = weighted / jnp.sum(weighted, axis=1, keepdims=True)
        return (weighted, weighted.astype(jnp.bfloat16))

    return lax.scan(advance, state, (haplos, observed, rates))


def backward_pass(state, haplos, observed, rates):
    total_haps = haplos.shape[1]

    def retreat(carry, inputs):
        allele_row, observed_col, rate = inputs
        kept = carry.astype(jnp.bfloat16)
        weighted = emission(allele_row, observed_col) * carry
        mixed = (1.0 - rate) * weighted + rate / total_haps * jnp.sum(
            weighted, axis=1, keepdims=True
        )
        mixed = mixed / jnp.sum(mixed, axis=1, keepdims=True)
        return (mixed, kept)

    return lax.scan(retreat, state, (haplos, observed, rates), reverse=True)


def keep_state(operands):
    return operands


def finish_dosage(forward_store, backward_store, haplos):
    allele_half = haplos.astype(jnp.bfloat16)
    carrying = backward_store * allele_half[:, None, :]
    numer = jnp.einsum("mtk,mtk->mt", forward_store, carrying, preferred_element_type=jnp.float32)
    denom = jnp.einsum(
        "mtk,mtk->mt", forward_store, backward_store, preferred_element_type=jnp.float32
    )
    return numer / denom


def local(alleles, observed, map_steps, start_weights, end_weights):
    packed = gather_directly(alleles, "hap", 1)
    start_rows = start_weights / jnp.sum(start_weights, axis=1, keepdims=True)
    end_rows = end_weights / jnp.sum(end_weights, axis=1, keepdims=True)
    position = lax.axis_index("grp")
    groups = lax.axis_size("grp")
    is_first = position == 0
    is_last = position == groups - 1
    targets = observed.shape[1]
    local_markers = observed.shape[0]
    haplos = unpack_alleles(packed)
    rates = 1.0 - jnp.exp(-map_steps.astype(jnp.float32) / map_unit)
    store_shape = (local_markers, targets, haplos.shape[1])
    forward_store = jnp.zeros(store_shape, jnp.bfloat16)
    backward_store = jnp.zeros(store_shape, jnp.bfloat16)

    def run_forward(operands):
        incoming, kept = operands
        begin = jnp.where(is_first, start_rows, incoming)
        return forward_pass(begin, haplos, observed, rates)

    def run_backward(operands):
        incoming, kept = operands
        begin = jnp.where(is_last, end_rows, incoming)
        return backward_pass(begin, haplos, observed, rates)

    def sweep_turn(section, carry):
        forward_in, backward_in, forward_kept, backward_kept = carry
        forward_out, forward_kept = lax.cond(
            section == position, run_forward, keep_state, (forward_in, forward_kept)
        )
        backward_out, backward_kept = lax.cond(
            section == groups - 1 - position, run_backward, keep_state, (backward_in, backward_kept)
        )
        forward_next = passed_along(forward_out, "grp", 1)
        backward_next = passed_along(backward_out, "grp", -1)
        return (forward_next, backward_next, forward_kept, backward_kept)

    result = lax.fori_loop(
        0, groups, sweep_turn, (start_rows, end_rows, forward_store, backward_store)
    )
    return finish_dosage(result[2], result[3], haplos)


def solution(mesh):
    in_specs = (P("grp", "hap"), P("grp", "hap"), P("grp"), P("hap", None), P("hap", None))
    out_specs = P("grp", "hap")
    return jax.shard_map(local, mesh=mesh, in_specs=in_specs, out_specs=out_specs, check_vma=False)
```

profile of v0, /device:TPU:1, one launch (start us, length us, event | category | flops | bytes accessed | tf_op | source)
XLA Modules:
  0.0 1186.3 jit_solution(277790262459155913)
XLA Ops:
  1.5 10.5 all-to-all-start
  16.0 4.8 all-to-all-done
  22.5 3.5 shift_right_arithmetic.27
  26.0 3.9 shift_right_arithmetic.28
  33.5 1147.2 %while.49 = (s32[]{:T(128)}, f32[4,15360]{1,0:T(4,128)S(1)}, f32[4,15360]{1,0:T(4,128)S(1)}, bf16[15,4,15360]{2,1,0:T(4,128)(2,1)}, bf16[15,4,15360]{2,1,0:T(4,1...) while((s32[]{:T(128)}, f32[4,15360]{1,0:T(4,128)S(1)}, ...), condition=%wide.region_15.16_spmd.clone, body=%wide.region_2.15_spmd.clone.sunk | while | flops 2688047 | bytes 15024031 | solution.py:127
  36.9 3.9 shift_right_arithmetic.60
  40.9 6.0 collective-permute-start
  47.0 48.0 %collective-permute-start.1 = (f32[4,15360]{1,0:T(4,128)S(1)}, f32[4,15360]{1,0:T(4,128)S(1)}, u32[]{:S(2)}, u32[]{:S(2)}) collective-permute-start(f32[4,15360]{1,0:T(4,128)S(1)} %get-tuple-element.830), channel_id=1, source_target_pairs={{32,0},{64,32},{96,64},{128,96},{160,128},{192,160},{224,192},{256... | collective-permute-start | bytes 737288 | tf_op jit(solution)/shard_map/while/body/eval_jaxpr/ppermute | solution.py:30
  96.2 3.5 shift_right_arithmetic.59
  99.6 3.9 shift_right_arithmetic.60
  103.6 48.8 %conditional.6 = ((f32[4,15360]{1,0:T(4,128)S(1)}, bf16[15,4,15360]{2,1,0:T(4,128)(2,1)})) conditional(s32[]{:T(128)} %convert_element_type.150, (f32[4,15360]{1,0:T(4,128)S(1)}, bf16[15,4,15360]{2,1,0:T(4,128)(2,1)}) %tuple.121, (pred[]{:T(512)}, f32[4,15360]{1,0:T(4,128)S(1)}, f32[4,15360]{1,0:T(4,128)S(1)}, s32[15,4]{1,0:T(8,128)S(1)}, ...), branch_computations={%region_3.0_spmd, %region_4.8_spmd} | conditional | flops 936980 | bytes 2397182 | solution.py:117
  103.7 48.6 %while.47 = (s32[]{:T(128)}, f32[4,15360]{1,0:T(4,128)S(1)}, bf16[15,4,15360]{2,1,0:T(4,128)(2,1)}, s32[15,4]{1,0:T(8,128)S(1)}, f32[15,15360]{1,0:T(8,128)S(1)}...) while((s32[]{:T(128)}, f32[4,15360]{1,0:T(4,128)S(1)}, ...), condition=%wide.region_8.7_spmd, body=%wide.region_5.6_spmd.sunk | while | flops 875540 | bytes 1659789 | solution.py:56
  157.4 4.4 collective-permute-done.1
  161.9 3.5 shift_right_arithmetic.59
  165.4 3.9 shift_right_arithmetic.60
  169.4 50.5 %collective-permute-start = (f32[4,15360]{1,0:T(4,128)S(1)}, f32[4,15360]{1,0:T(4,128)S(1)}, u32[]{:S(2)}, u32[]{:S(2)}) collective-permute-start(f32[4,15360]{1,0:T(4,128)S(1)} %get-tuple-element.829), channel_id=1, source_target_pairs={{0,32},{32,64},{64,96},{96,128},{128,160},{160,192},{192,224},{224... | collective-permute-start | bytes 737288 | tf_op jit(solution)/shard_map/while/body/eval_jaxpr/ppermute | solution.py:30
  223.0 4.4 collective-permute-done.1
  227.4 3.5 shift_right_arithmetic.59
  230.9 3.9 shift_right_arithmetic.60
  240.0 47.4 %collective-permute-done.1 = f32[4,15360]{1,0:T(4,128)S(1)} collective-permute-done((f32[4,15360]{1,0:T(4,128)S(1)}, f32[4,15360]{1,0:T(4,128)S(1)}, u32[]{:S(2)}, u32[]{:S(2)}) %collective-permute-start.1) | collective-permute-done | bytes 245792 | tf_op jit(solution)/shard_map/while/body/eval_jaxpr/ppermute | solution.py:30
  287.4 3.5 shift_right_arithmetic.59
  290.9 3.9 shift_right_arithmetic.60
  300.0 4.4 collective-permute-done.1
  304.4 3.5 shift_right_arithmetic.59
  307.9 3.9 shift_right_arithmetic.60
  311.9 47.6 %collective-permute-start = (f32[4,15360]{1,0:T(4,128)S(1)}, f32[4,15360]{1,0:T(4,128)S(1)}, u32[]{:S(2)}, u32[]{:S(2)}) collective-permute-start(f32[4,15360]{1,0:T(4,128)S(1)} %get-tuple-element.829), channel_id=1, source_target_pairs={{0,32},{32,64},{64,96},{96,128},{128,160},{160,192},{192,224},{224... | collective-permute-start | bytes 737288 | tf_op jit(solution)/shard_map/while/body/eval_jaxpr/ppermute | solution.py:30
  362.7 7.3 collective-permute-done.1
  370.0 3.5 shift_right_arithmetic.59
  373.5 3.9 shift_right_arithmetic.60
  382.5 47.4 %collective-permute-done.1 = f32[4,15360]{1,0:T(4,128)S(1)} collective-permute-done((f32[4,15360]{1,0:T(4,128)S(1)}, f32[4,15360]{1,0:T(4,128)S(1)}, u32[]{:S(2)}, u32[]{:S(2)}) %collective-permute-start.1) | collective-permute-done | bytes 245792 | tf_op jit(solution)/shard_map/while/body/eval_jaxpr/ppermute | solution.py:30
  430.0 3.5 shift_right_arithmetic.59
  433.5 3.9 shift_right_arithmetic.60
  442.6 4.4 collective-permute-done.1
  447.0 3.5 shift_right_arithmetic.59
  450.5 3.9 shift_right_arithmetic.60
  454.5 44.7 %collective-permute-start = (f32[4,15360]{1,0:T(4,128)S(1)}, f32[4,15360]{1,0:T(4,128)S(1)}, u32[]{:S(2)}, u32[]{:S(2)}) collective-permute-start(f32[4,15360]{1,0:T(4,128)S(1)} %get-tuple-element.829), channel_id=1, source_target_pairs={{0,32},{32,64},{64,96},{96,128},{128,160},{160,192},{192,224},{224... | collective-permute-start | bytes 737288 | tf_op jit(solution)/shard_map/while/body/eval_jaxpr/ppermute | solution.py:30
  502.4 10.2 collective-permute-done.1
  512.5 3.5 shift_right_arithmetic.59
  516.0 3.9 shift_right_arithmetic.60
  525.1 47.4 %collective-permute-done.1 = f32[4,15360]{1,0:T(4,128)S(1)} collective-permute-done((f32[4,15360]{1,0:T(4,128)S(1)}, f32[4,15360]{1,0:T(4,128)S(1)}, u32[]{:S(2)}, u32[]{:S(2)}) %collective-permute-start.1) | collective-permute-done | bytes 245792 | tf_op jit(solution)/shard_map/while/body/eval_jaxpr/ppermute | solution.py:30
  572.5 3.5 shift_right_arithmetic.59
  576.0 3.9 shift_right_arithmetic.60
  585.1 49.0 %collective-permute-done.1 = f32[4,15360]{1,0:T(4,128)S(1)} collective-permute-done((f32[4,15360]{1,0:T(4,128)S(1)}, f32[4,15360]{1,0:T(4,128)S(1)}, u32[]{:S(2)}, u32[]{:S(2)}) %collective-permute-start.1) | collective-permute-done | bytes 245792 | tf_op jit(solution)/shard_map/while/body/eval_jaxpr/ppermute | solution.py:30
  634.1 3.5 shift_right_arithmetic.59
  637.6 3.9 shift_right_arithmetic.60
  641.6 93.8 %collective-permute-start = (f32[4,15360]{1,0:T(4,128)S(1)}, f32[4,15360]{1,0:T(4,128)S(1)}, u32[]{:S(2)}, u32[]{:S(2)}) collective-permute-start(f32[4,15360]{1,0:T(4,128)S(1)} %get-tuple-element.829), channel_id=1, source_target_pairs={{0,32},{32,64},{64,96},{96,128},{128,160},{160,192},{192,224},{224... | collective-permute-start | bytes 737288 | tf_op jit(solution)/shard_map/while/body/eval_jaxpr/ppermute | solution.py:30
  738.6 66.2 %collective-permute-done.1 = f32[4,15360]{1,0:T(4,128)S(1)} collective-permute-done((f32[4,15360]{1,0:T(4,128)S(1)}, f32[4,15360]{1,0:T(4,128)S(1)}, u32[]{:S(2)}, u32[]{:S(2)}) %collective-permute-start.1) | collective-permute-done | bytes 245792 | tf_op jit(solution)/shard_map/while/body/eval_jaxpr/ppermute | solution.py:30
  804.8 3.5 shift_right_arithmetic.59
  808.3 3.9 shift_right_arithmetic.60
  812.3 48.1 %collective-permute-start = (f32[4,15360]{1,0:T(4,128)S(1)}, f32[4,15360]{1,0:T(4,128)S(1)}, u32[]{:S(2)}, u32[]{:S(2)}) collective-permute-start(f32[4,15360]{1,0:T(4,128)S(1)} %get-tuple-element.829), channel_id=1, source_target_pairs={{0,32},{32,64},{64,96},{96,128},{128,160},{160,192},{192,224},{224... | collective-permute-start | bytes 737288 | tf_op jit(solution)/shard_map/while/body/eval_jaxpr/ppermute | solution.py:30
  863.6 62.1 %collective-permute-done.1 = f32[4,15360]{1,0:T(4,128)S(1)} collective-permute-done((f32[4,15360]{1,0:T(4,128)S(1)}, f32[4,15360]{1,0:T(4,128)S(1)}, u32[]{:S(2)}, u32[]{:S(2)}) %collective-permute-start.1) | collective-permute-done | bytes 245792 | tf_op jit(solution)/shard_map/while/body/eval_jaxpr/ppermute | solution.py:30
  925.8 3.5 shift_right_arithmetic.59
  929.2 3.9 shift_right_arithmetic.60
  933.2 51.0 %collective-permute-start = (f32[4,15360]{1,0:T(4,128)S(1)}, f32[4,15360]{1,0:T(4,128)S(1)}, u32[]{:S(2)}, u32[]{:S(2)}) collective-permute-start(f32[4,15360]{1,0:T(4,128)S(1)} %get-tuple-element.829), channel_id=1, source_target_pairs={{0,32},{32,64},{64,96},{96,128},{128,160},{160,192},{192,224},{224... | collective-permute-start | bytes 737288 | tf_op jit(solution)/shard_map/while/body/eval_jaxpr/ppermute | solution.py:30
  987.4 59.2 %collective-permute-done.1 = f32[4,15360]{1,0:T(4,128)S(1)} collective-permute-done((f32[4,15360]{1,0:T(4,128)S(1)}, f32[4,15360]{1,0:T(4,128)S(1)}, u32[]{:S(2)}, u32[]{:S(2)}) %collective-permute-start.1) | collective-permute-done | bytes 245792 | tf_op jit(solution)/shard_map/while/body/eval_jaxpr/ppermute | solution.py:30
  1046.7 3.5 shift_right_arithmetic.59
  1050.2 3.9 shift_right_arithmetic.60
  1056.1 52.0 %conditional.7 = ((f32[4,15360]{1,0:T(4,128)S(1)}, bf16[15,4,15360]{2,1,0:T(4,128)(2,1)})) conditional(s32[]{:T(128)} %convert_element_type.151, (f32[4,15360]{1,0:T(4,128)S(1)}, bf16[15,4,15360]{2,1,0:T(4,128)(2,1)}) %tuple.123, (pred[]{:T(512)}, f32[4,15360]{1,0:T(4,128)S(1)}, f32[4,15360]{1,0:T(4,128)S(1)}, f32[15]{0:T(128)S(1)}, ...), branch_computations={%region_9.9_spmd, %region_10.14_spmd} | conditional | flops 1059861 | bytes 4977184 | solution.py:120
  1057.9 50.1 %while.48 = (s32[]{:T(128)}, f32[4,15360]{1,0:T(4,128)S(1)}, bf16[15,4,15360]{2,1,0:T(4,128)(2,1)}, f32[15]{0:T(128)S(1)}, s32[15,4]{1,0:T(8,128)S(1)}, /*index=...) while((s32[]{:T(128)}, f32[4,15360]{1,0:T(4,128)S(1)}, ...), condition=%wide.region_14.13_spmd, body=%wide.region_11.12_spmd.sunk | while | flops 998421 | bytes 2396589 | solution.py:72
  1110.1 5.6 collective-permute-done.1
  1115.6 3.5 shift_right_arithmetic.59
  1119.1 3.9 shift_right_arithmetic.60
  1125.1 54.4 %collective-permute-start.1 = (f32[4,15360]{1,0:T(4,128)S(1)}, f32[4,15360]{1,0:T(4,128)S(1)}, u32[]{:S(2)}, u32[]{:S(2)}) collective-permute-start(f32[4,15360]{1,0:T(4,128)S(1)} %get-tuple-element.830), channel_id=1, source_target_pairs={{32,0},{64,32},{96,64},{128,96},{160,128},{192,160},{224,192},{256... | collective-permute-start | bytes 737288 | tf_op jit(solution)/shard_map/while/body/eval_jaxpr/ppermute | solution.py:30
  1180.6 4.9 fusion.7
  (375 shorter events, 145.0 us)
Async XLA Ops:
  0.0 15.6 %copy-start.1 = (s32[15]{0:T(128)S(1)}, s32[15]{0:T(128)}, u32[]{:S(2)}) copy-start(s32[15]{0:T(128)} %param.17) | copy-start | bytes 184
  0.0 15.9 %copy-start = (s32[15,4]{0,1:T(4,128)S(1)}, s32[15,4]{0,1:T(4,128)}, u32[]{:S(2)}) copy-start(s32[15,4]{0,1:T(4,128)} %param.16) | copy-start | bytes 724
  1.5 19.3 %all-to-all-start = ((s32[32,1,240]{2,1,0:T(1,128)}), s32[32,1,240]{2,1,0:T(1,128)S(1)}, u32[]{:S(2)}, u32[]{:S(2)}) async-start(s32[32,1,240]{2,1,0:T(1,128)} %reshape.122), calls=%async_computation | async-start | bytes 65536 | tf_op jit(solution)/shard_map/all_to_all | solution.py:18
  40.9 54.1 %collective-permute-start = (f32[4,15360]{1,0:T(4,128)S(1)}, f32[4,15360]{1,0:T(4,128)S(1)}, u32[]{:S(2)}, u32[]{:S(2)}) collective-permute-start(f32[4,15360]{1,0:T(4,128)S(1)} %get-tuple-element.829), channel_id=1, source_target_pairs={{0,32},{32,64},{64,96},{96,128},{128,160},{160,192},{192,224},{224... | collective-permute-start | bytes 737288 | tf_op jit(solution)/shard_map/while/body/eval_jaxpr/ppermute | solution.py:30
  47.0 49.2 %collective-permute-start.1 = (f32[4,15360]{1,0:T(4,128)S(1)}, f32[4,15360]{1,0:T(4,128)S(1)}, u32[]{:S(2)}, u32[]{:S(2)}) collective-permute-start(f32[4,15360]{1,0:T(4,128)S(1)} %get-tuple-element.830), channel_id=1, source_target_pairs={{32,0},{64,32},{96,64},{128,96},{160,128},{192,160},{224,192},{256... | collective-permute-start | bytes 737288 | tf_op jit(solution)/shard_map/while/body/eval_jaxpr/ppermute | solution.py:30
  152.4 5.0 collective-permute-start
  154.3 7.5 collective-permute-start.1
  169.4 53.6 %collective-permute-start = (f32[4,15360]{1,0:T(4,128)S(1)}, f32[4,15360]{1,0:T(4,128)S(1)}, u32[]{:S(2)}, u32[]{:S(2)}) collective-permute-start(f32[4,15360]{1,0:T(4,128)S(1)} %get-tuple-element.829), channel_id=1, source_target_pairs={{0,32},{32,64},{64,96},{96,128},{128,160},{160,192},{192,224},{224... | collective-permute-start | bytes 737288 | tf_op jit(solution)/shard_map/while/body/eval_jaxpr/ppermute | solution.py:30
  219.9 7.5 collective-permute-start.1
  234.9 5.0 collective-permute-start
  236.9 50.5 %collective-permute-start.1 = (f32[4,15360]{1,0:T(4,128)S(1)}, f32[4,15360]{1,0:T(4,128)S(1)}, u32[]{:S(2)}, u32[]{:S(2)}) collective-permute-start(f32[4,15360]{1,0:T(4,128)S(1)} %get-tuple-element.830), channel_id=1, source_target_pairs={{32,0},{64,32},{96,64},{128,96},{160,128},{192,160},{224,192},{256... | collective-permute-start | bytes 737288 | tf_op jit(solution)/shard_map/while/body/eval_jaxpr/ppermute | solution.py:30
  294.9 5.0 collective-permute-start
  296.9 7.5 collective-permute-start.1
  311.9 50.7 %collective-permute-start = (f32[4,15360]{1,0:T(4,128)S(1)}, f32[4,15360]{1,0:T(4,128)S(1)}, u32[]{:S(2)}, u32[]{:S(2)}) collective-permute-start(f32[4,15360]{1,0:T(4,128)S(1)} %get-tuple-element.829), channel_id=1, source_target_pairs={{0,32},{32,64},{64,96},{96,128},{128,160},{160,192},{192,224},{224... | collective-permute-start | bytes 737288 | tf_op jit(solution)/shard_map/while/body/eval_jaxpr/ppermute | solution.py:30
  359.6 10.4 collective-permute-start.1
  377.5 5.0 collective-permute-start
  379.4 50.5 %collective-permute-start.1 = (f32[4,15360]{1,0:T(4,128)S(1)}, f32[4,15360]{1,0:T(4,128)S(1)}, u32[]{:S(2)}, u32[]{:S(2)}) collective-permute-start(f32[4,15360]{1,0:T(4,128)S(1)} %get-tuple-element.830), channel_id=1, source_target_pairs={{32,0},{64,32},{96,64},{128,96},{160,128},{192,160},{224,192},{256... | collective-permute-start | bytes 737288 | tf_op jit(solution)/shard_map/while/body/eval_jaxpr/ppermute | solution.py:30
  437.5 5.0 collective-permute-start
  439.4 7.5 collective-permute-start.1
  454.5 47.8 %collective-permute-start = (f32[4,15360]{1,0:T(4,128)S(1)}, f32[4,15360]{1,0:T(4,128)S(1)}, u32[]{:S(2)}, u32[]{:S(2)}) collective-permute-start(f32[4,15360]{1,0:T(4,128)S(1)} %get-tuple-element.829), channel_id=1, source_target_pairs={{0,32},{32,64},{64,96},{96,128},{128,160},{160,192},{192,224},{224... | collective-permute-start | bytes 737288 | tf_op jit(solution)/shard_map/while/body/eval_jaxpr/ppermute | solution.py:30
  499.2 13.3 %collective-permute-start.1 = (f32[4,15360]{1,0:T(4,128)S(1)}, f32[4,15360]{1,0:T(4,128)S(1)}, u32[]{:S(2)}, u32[]{:S(2)}) collective-permute-start(f32[4,15360]{1,0:T(4,128)S(1)} %get-tuple-element.830), channel_id=1, source_target_pairs={{32,0},{64,32},{96,64},{128,96},{160,128},{192,160},{224,192},{256... | collective-permute-start | bytes 737288 | tf_op jit(solution)/shard_map/while/body/eval_jaxpr/ppermute | solution.py:30
  520.0 5.0 collective-permute-start
  522.0 50.5 %collective-permute-start.1 = (f32[4,15360]{1,0:T(4,128)S(1)}, f32[4,15360]{1,0:T(4,128)S(1)}, u32[]{:S(2)}, u32[]{:S(2)}) collective-permute-start(f32[4,15360]{1,0:T(4,128)S(1)} %get-tuple-element.830), channel_id=1, source_target_pairs={{32,0},{64,32},{96,64},{128,96},{160,128},{192,160},{224,192},{256... | collective-permute-start | bytes 737288 | tf_op jit(solution)/shard_map/while/body/eval_jaxpr/ppermute | solution.py:30
  580.0 5.0 collective-permute-start
  582.0 52.1 %collective-permute-start.1 = (f32[4,15360]{1,0:T(4,128)S(1)}, f32[4,15360]{1,0:T(4,128)S(1)}, u32[]{:S(2)}, u32[]{:S(2)}) collective-permute-start(f32[4,15360]{1,0:T(4,128)S(1)} %get-tuple-element.830), channel_id=1, source_target_pairs={{32,0},{64,32},{96,64},{128,96},{160,128},{192,160},{224,192},{256... | collective-permute-start | bytes 737288 | tf_op jit(solution)/shard_map/while/body/eval_jaxpr/ppermute | solution.py:30
  641.6 96.9 %collective-permute-start = (f32[4,15360]{1,0:T(4,128)S(1)}, f32[4,15360]{1,0:T(4,128)S(1)}, u32[]{:S(2)}, u32[]{:S(2)}) collective-permute-start(f32[4,15360]{1,0:T(4,128)S(1)} %get-tuple-element.829), channel_id=1, source_target_pairs={{0,32},{32,64},{64,96},{96,128},{128,160},{160,192},{192,224},{224... | collective-permute-start | bytes 737288 | tf_op jit(solution)/shard_map/while/body/eval_jaxpr/ppermute | solution.py:30
  735.5 69.3 %collective-permute-start.1 = (f32[4,15360]{1,0:T(4,128)S(1)}, f32[4,15360]{1,0:T(4,128)S(1)}, u32[]{:S(2)}, u32[]{:S(2)}) collective-permute-start(f32[4,15360]{1,0:T(4,128)S(1)} %get-tuple-element.830), channel_id=1, source_target_pairs={{32,0},{64,32},{96,64},{128,96},{160,128},{192,160},{224,192},{256... | collective-permute-start | bytes 737288 | tf_op jit(solution)/shard_map/while/body/eval_jaxpr/ppermute | solution.py:30
  812.3 51.3 %collective-permute-start = (f32[4,15360]{1,0:T(4,128)S(1)}, f32[4,15360]{1,0:T(4,128)S(1)}, u32[]{:S(2)}, u32[]{:S(2)}) collective-permute-start(f32[4,15360]{1,0:T(4,128)S(1)} %get-tuple-element.829), channel_id=1, source_target_pairs={{0,32},{32,64},{64,96},{96,128},{128,160},{160,192},{192,224},{224... | collective-permute-start | bytes 737288 | tf_op jit(solution)/shard_map/while/body/eval_jaxpr/ppermute | solution.py:30
  860.5 65.2 %collective-permute-start.1 = (f32[4,15360]{1,0:T(4,128)S(1)}, f32[4,15360]{1,0:T(4,128)S(1)}, u32[]{:S(2)}, u32[]{:S(2)}) collective-permute-start(f32[4,15360]{1,0:T(4,128)S(1)} %get-tuple-element.830), channel_id=1, source_target_pairs={{32,0},{64,32},{96,64},{128,96},{160,128},{192,160},{224,192},{256... | collective-permute-start | bytes 737288 | tf_op jit(solution)/shard_map/while/body/eval_jaxpr/ppermute | solution.py:30
  933.2 54.1 %collective-permute-start = (f32[4,15360]{1,0:T(4,128)S(1)}, f32[4,15360]{1,0:T(4,128)S(1)}, u32[]{:S(2)}, u32[]{:S(2)}) collective-permute-start(f32[4,15360]{1,0:T(4,128)S(1)} %get-tuple-element.829), channel_id=1, source_target_pairs={{0,32},{32,64},{64,96},{96,128},{128,160},{160,192},{192,224},{224... | collective-permute-start | bytes 737288 | tf_op jit(solution)/shard_map/while/body/eval_jaxpr/ppermute | solution.py:30
  984.3 62.4 %collective-permute-start.1 = (f32[4,15360]{1,0:T(4,128)S(1)}, f32[4,15360]{1,0:T(4,128)S(1)}, u32[]{:S(2)}, u32[]{:S(2)}) collective-permute-start(f32[4,15360]{1,0:T(4,128)S(1)} %get-tuple-element.830), channel_id=1, source_target_pairs={{32,0},{64,32},{96,64},{128,96},{160,128},{192,160},{224,192},{256... | collective-permute-start | bytes 737288 | tf_op jit(solution)/shard_map/while/body/eval_jaxpr/ppermute | solution.py:30
  1054.2 55.9 %collective-permute-start = (f32[4,15360]{1,0:T(4,128)S(1)}, f32[4,15360]{1,0:T(4,128)S(1)}, u32[]{:S(2)}, u32[]{:S(2)}) collective-permute-start(f32[4,15360]{1,0:T(4,128)S(1)} %get-tuple-element.829), channel_id=1, source_target_pairs={{0,32},{32,64},{64,96},{96,128},{128,160},{160,192},{192,224},{224... | collective-permute-start | bytes 737288 | tf_op jit(solution)/shard_map/while/body/eval_jaxpr/ppermute | solution.py:30
  1108.1 7.5 collective-permute-start.1
  1123.1 56.3 %collective-permute-start = (f32[4,15360]{1,0:T(4,128)S(1)}, f32[4,15360]{1,0:T(4,128)S(1)}, u32[]{:S(2)}, u32[]{:S(2)}) collective-permute-start(f32[4,15360]{1,0:T(4,128)S(1)} %get-tuple-element.829), channel_id=1, source_target_pairs={{0,32},{32,64},{64,96},{96,128},{128,160},{160,192},{192,224},{224... | collective-permute-start | bytes 737288 | tf_op jit(solution)/shard_map/while/body/eval_jaxpr/ppermute | solution.py:30
  1125.1 55.5 %collective-permute-start.1 = (f32[4,15360]{1,0:T(4,128)S(1)}, f32[4,15360]{1,0:T(4,128)S(1)}, u32[]{:S(2)}, u32[]{:S(2)}) collective-permute-start(f32[4,15360]{1,0:T(4,128)S(1)} %get-tuple-element.830), channel_id=1, source_target_pairs={{32,0},{64,32},{96,64},{128,96},{160,128},{192,160},{224,192},{256... | collective-permute-start | bytes 737288 | tf_op jit(solution)/shard_map/while/body/eval_jaxpr/ppermute | solution.py:30
where the time goes:
time: 1190 us
  starting transfers between devices  502 us (42%)
  waiting for transfers between devices  438 us (37%)
  local copies, waits for them, and re-layouts  151 us (13%)
  other arithmetic  58.3 us (5%)
  loops' own time  36.5 us (3%)
    ppermute x32, starting transfers between devices, passed_along(): lax.ppermute(value, axis, [(source, source + steps) for source in range(i...  492 us
    ppermute x32, waiting for transfers between devices, passed_along(): lax.ppermute(value, axis, [(source, source + steps) for source in range(i...  433 us
    shift_right_arithmetic x37, local copies, waits for them, and re-layouts, unpack_alleles(): jnp.right_shift(packed[:, :, None], shifts[None, None, :])  125 us
  transfers between devices with their start and end apart: 33, of which 30 were waited for; matrix products, arithmetic and copies ran while one was open for 3% of the time, Pallas kernels for 0%

commit v1 on v0

v1 whole, which is shorter than its diff:
```python
import functools

import jax
import jax.numpy as jnp
from jax import lax
from jax.experimental import pallas as pl
from jax.experimental.pallas import tpu as pltpu
from jax.sharding import Mesh, PartitionSpec as P

K = 15360
MARKERS = 240
GROUPS = 16
SPAN = 15
TILES = 15
TGT = 4
BLOCKS = MARKERS // 3
LANES = 128
MSG = 384
hit = 0.99
miss = 0.01
map_unit = 100000.0
lift = float(2**60)


def full(value):
    return jnp.broadcast_to(value, (8, LANES))


def total(tile):
    rows = jnp.sum(tile, axis=0, keepdims=True)
    return full(jnp.sum(rows, axis=1, keepdims=True))


def swapped_blocks(tiles, lane):
    tiles = list(tiles)
    for step in (1, 2, 4):
        low = (lane & (16 * step)) == 0
        for j in range(8):
            if j & step:
                continue
            first, second = tiles[j], tiles[j + step]
            tiles[j] = jnp.where(low, first, pltpu.roll(second, 16 * step, 1))
            tiles[j + step] = jnp.where(low, pltpu.roll(first, LANES - 16 * step, 1), second)
    return tiles


def kernel(place, beta, keep, em, own, other, weights_start, weights_end, emv, out,
           words, fwd, bwd, fstore, bstore, counts_in, sums, gv, gs, nd, sem):
    group = place[0]
    core = lax.rem(group, 2)
    lane = lax.broadcasted_iota(jnp.int32, (8, LANES), 1)
    upper = lax.broadcasted_iota(jnp.int32, (8, LANES), 0) < 4

    def unpack(z, carry):
        for ref, which in ((own, core), (other, 1 - core)):
            tiles = []
            for j in range(8):
                parts = [ref[pl.ds(j * 24 + z * 3 + a, 4, stride=192), :] for a in range(2)]
                tiles.append(jnp.concatenate(parts, axis=0))
            tiles = swapped_blocks(tiles, lane)
            first = (2 * z + which) * SPAN
            for m in range(SPAN):
                tile = tiles[m % 8]
                turned = pltpu.roll(tile, 4, 0)
                low, high = (tile, turned) if m < 8 else (turned, tile)
                words[first + m] = jnp.where(upper, low, lax.shift_right_logical(high, 15))
        return carry

    lax.fori_loop(0, 8, unpack, 0)

    def count(block, carry):
        w0, w1, w2 = [words[3 * block + j] & 0x7FFF for j in range(3)]
        w01, w12, w02 = w0 & w1, w1 & w2, w0 & w2
        for q, w in enumerate((w0, w1, w2, w01, w12, w02, w01 & w2)):
            ones = lax.population_count(w).astype(jnp.float32)
            counts_in[q, pl.ds(block, 1), :] = jnp.sum(ones, axis=0, keepdims=True)
        return carry

    lax.fori_loop(0, BLOCKS, count, 0)
    ones = jnp.ones((8, LANES), jnp.bfloat16)
    n = []
    for q in range(7):
        table = counts_in[q].astype(jnp.bfloat16)
        n.append(lax.dot_general(ones, table, (((1,), (1,)), ((), ())), preferred_element_type=jnp.float32))
    n0, n1, n2, n01, n12, n02, n012 = n
    a1, a0, b1, b0, c1, c0 = [emv[j] for j in range(6)]

    def pair(x1, x0, y1, y0, nx, ny, nxy):
        return nxy * (x1 * y1) + (nx - nxy) * (x1 * y0) + (ny - nxy) * (x0 * y1) + (K - nx - ny + nxy) * (x0 * y0)

    gv[0:8, :] = n0 * a1 + (K - n0) * a0
    gv[8:16, :] = n1 * b1 + (K - n1) * b0
    gv[16:24, :] = n2 * c1 + (K - n2) * c0
    gv[24:32, :] = pair(a1, a0, b1, b0, n0, n1, n01)
    gv[32:40, :] = pair(b1, b0, c1, c0, n1, n2, n12)
    with_a = n012 * (b1 * c1) + (n01 - n012) * (b1 * c0) + (n02 - n012) * (b0 * c1) + (n0 - n01 - n02 + n012) * (b0 * c0)
    rest = (n12 - n012) * (b1 * c1) + (n1 - n01 - n12 + n012) * (b1 * c0) + (n2 - n02 - n12 + n012) * (b0 * c1) \
        + (K - n0 - n1 - n2 + n01 + n12 + n02 - n012) * (b0 * c0)
    gv[40:48, :] = a1 * with_a + a0 * rest
    copy = pltpu.make_async_copy(gv, gs, sem)
    copy.start()
    copy.wait()

    for t in range(TGT):
        for v in range(TILES):
            fwd[t, v] = weights_start[t, v]
            bwd[t, v] = weights_end[t, v]

    def sum_of(ref):
        sums_now = []
        for t in range(TGT):
            acc = ref[t, 0]
            for v in range(1, TILES):
                acc = acc + ref[t, v]
            sums_now.append(total(acc))
        return tuple(sums_now)

    def three(state, block, carry, reverse):
        order = (2, 1, 0) if reverse else (0, 1, 2)
        shift = 1 if reverse else 0
        marks = [3 * block + j for j in order]
        tile_words = [words[m] for m in marks]
        rates = [beta[m + shift] for m in marks]
        singles = order
        pairs = (4, 3) if reverse else (3, 4)
        result = [None] * TGT
        new_scale = [jnp.ones((8, LANES), jnp.float32)] * TGT
        for half in range(2):
            pass
        sums_of = {}
        emis = {t: [(em[m * 8 + 2 * t], em[m * 8 + 2 * t + 1]) for m in marks] for t in range(TGT)}

        def down(targets):
            accs = {t: [None] * 3 for t in targets}
            first = {t: (emis[t][0][0] * carry[4 + t], emis[t][0][1] * carry[4 + t]) for t in targets}
            for v in range(TILES):
                masks = [(w & (1 << v)) != 0 for w in tile_words]
                for t in targets:
                    y = state[t, v]
                    for j in range(3):
                        e1, e0 = first[t] if j == 0 else emis[t][j]
                        y = y * jnp.where(masks[j], e1, e0)
                        accs[t][j] = y if v == 0 else accs[t][j] + y
                    state[t, v] = y
            for t in targets:
                sums_of[t] = [total(a) for a in accs[t]]

        def up(targets):
            mix = {}
            for t in targets:
                q1, q2, q3 = sums_of[t]
                g = lambda q: gs[8 * q + t, block]
                m0 = rates[0] * (carry[t] * carry[4 + t])
                s1 = q1 + m0 * g(singles[0])
                m1 = rates[1] * s1
                s2 = (q2 + m0 * g(pairs[0])) + m1 * g(singles[1])
                m2 = rates[2] * s2
                s3 = (q3 + m0 * g(5)) + m1 * g(pairs[1]) + m2 * g(singles[2])
                result[t] = s3
                mix[t] = (m0 * emis[t][0][0] + m1, m0 * emis[t][0][1] + m1, m2)
            for v in range(TILES):
                masks = [(w & (1 << v)) != 0 for w in tile_words]
                for t in targets:
                    h = jnp.where(masks[0], mix[t][0], mix[t][1])
                    h = h * jnp.where(masks[1], *emis[t][1]) + mix[t][2]
                    h = h * jnp.where(masks[2], *emis[t][2])
                    state[t, v] = state[t, v] + h

        down((0, 1))
        down((2, 3))
        up((0, 1))
        up((2, 3))
        return tuple(result) + tuple(new_scale)

    def run(state, first, count_groups, reverse):
        def one_group(i, sums_now):
            block = (first - i if reverse else first + i) * 5
            carry = tuple(sums_now) + tuple(lift / s for s in sums_now)
            def one_block(j, carry):
                return three(state, block + (4 - j if reverse else j), carry, reverse)
            return lax.fori_loop(0, 5, one_block, carry)[:TGT]
        return lax.fori_loop(0, count_groups, one_group, sum_of(state))

    fsum = run(fwd, 0, group, False)
    bsum = run(bwd, GROUPS - 1, GROUPS - 1 - group, True)

    begin = group * SPAN
    scale_f = tuple(lift / s for s in fsum)
    scale_b = tuple(lift / s for s in bsum)

    def own_step(i, carry):
        fs, bs, ff, bf = carry[0:4], carry[4:8], carry[8:12], carry[12:16]
        mf, mb = begin + i, begin + SPAN - 1 - i
        wf, wb = words[mf], words[mb]
        fnew, bnew = [], []
        for t in range(TGT):
            mix = beta[mf] * fs[t]
            e1, e0 = em[mf * 8 + 2 * t] * ff[t], em[mf * 8 + 2 * t + 1] * ff[t]
            acc = None
            for v in range(TILES):
                x = (fwd[t, v] + mix) * jnp.where((wf & (1 << v)) != 0, e1, e0)
                fwd[t, v] = x
                fstore[i * TGT + t, v] = x
                acc = x if v == 0 else acc + x
            fnew.append(acc)
        for t in range(TGT):
            mix = beta[mb + 1] * bs[t]
            e1, e0 = em[mb * 8 + 2 * t] * bf[t], em[mb * 8 + 2 * t + 1] * bf[t]
            sums[1, (SPAN - 1 - i) * TGT + t] = bs[t]
            acc = None
            for v in range(TILES):
                b = bwd[t, v] + mix
                bstore[(SPAN - 1 - i) * TGT + t, v] = b
                x = b * jnp.where((wb & (1 << v)) != 0, e1, e0)
                bwd[t, v] = x
                acc = x if v == 0 else acc + x
            bnew.append(acc)
        fnew = [total(a) for a in fnew]
        bnew = [total(a) for a in bnew]
        for t in range(TGT):
            sums[0, i * TGT + t] = fnew[t]
        one = jnp.ones((8, LANES), jnp.float32)
        return tuple(fnew) + tuple(bnew) + (one,) * 8

    lax.fori_loop(0, SPAN, own_step, tuple(fsum) + tuple(bsum) + scale_f + scale_b)

    def dose(i, carry):
        m = begin + i
        w = words[m]
        for t in range(TGT):
            row = i * TGT + t
            by_f = 1.0 / sums[0, row]
            by_b = keep[m + 1] / sums[1, row]
            num = den = None
            for v in range(TILES):
                f = (fstore[row, v] * by_f).astype(jnp.bfloat16).astype(jnp.float32)
                b = (bstore[row, v] * by_b).astype(jnp.bfloat16).astype(jnp.float32)
                p = f * b
                q = jnp.where((w & (1 << v)) != 0, p, 0.0)
                num = q if v == 0 else num + q
                den = p if v == 0 else den + p
            nd[0, t, pl.ds(i, 1), :] = jnp.sum(num, axis=0, keepdims=True)
            nd[1, t, pl.ds(i, 1), :] = jnp.sum(den, axis=0, keepdims=True)
        return carry

    lax.fori_loop(0, SPAN, dose, 0)
    column = lax.broadcasted_iota(jnp.int32, (SPAN, LANES), 1)
    answer = jnp.zeros((SPAN, LANES), jnp.float32)
    for t in range(TGT):
        num = jnp.sum(nd[0, t, 0:SPAN, :], axis=1, keepdims=True)
        den = jnp.sum(nd[1, t, 0:SPAN, :], axis=1, keepdims=True)
        answer = jnp.where(column == t, num / den, answer)
    out[...] = answer[:, 0:TGT]


def chains(place, beta, keep, em, own, other, weights_start, weights_end, emv):
    smem = pl.BlockSpec(memory_space=pltpu.SMEM)
    vmem = pl.BlockSpec(memory_space=pltpu.VMEM)
    f32 = jnp.float32
    return pl.pallas_call(
        kernel,
        out_shape=jax.ShapeDtypeStruct((SPAN, TGT), f32),
        in_specs=[smem] * 4 + [vmem] * 5,
        out_specs=vmem,
        scratch_shapes=[
            pltpu.VMEM((MARKERS, 8, LANES), jnp.int32),
            pltpu.VMEM((TGT, TILES, 8, LANES), f32),
            pltpu.VMEM((TGT, TILES, 8, LANES), f32),
            pltpu.VMEM((SPAN * TGT, TILES, 8, LANES), f32),
            pltpu.VMEM((SPAN * TGT, TILES, 8, LANES), f32),
            pltpu.VMEM((7, LANES, LANES), f32),
            pltpu.VMEM((2, SPAN * TGT, 8, LANES), f32),
            pltpu.VMEM((48, LANES), f32),
            pltpu.SMEM((48, LANES), f32),
            pltpu.VMEM((2, TGT, 16, LANES), f32),
            pltpu.SemaphoreType.DMA,
        ],
        compiler_params=pltpu.CompilerParams(vmem_limit_bytes=48 << 20),
    )(place, beta, keep, em, own, other, weights_start, weights_end, emv)


def to_all(array, axes):
    peers = 1
    for axis in axes:
        peers *= lax.axis_size(axis)
    return lax.all_to_all(jnp.broadcast_to(array[None], (peers, *array.shape)), axes, 0, 0, tiled=True)


def planes(weights):
    split = weights.reshape(TGT, 4, LANES, 2, 15)
    return split.transpose(0, 4, 3, 1, 2).reshape(TGT, TILES, 8, LANES)


def local(alleles, observed, map_steps, start_weights, end_weights):
    zero = jnp.zeros
    message = jnp.concatenate([
        alleles.reshape(1, 240), map_steps.reshape(1, 15), zero((1, 1), jnp.int32),
        observed.reshape(1, 60), zero((1, 68), jnp.int32)], axis=1)
    line = to_all(message, ("z",))
    spread = to_all(line.reshape(1, 8 * MSG), ("x", "y"))
    own = spread.reshape(768, LANES)
    other = lax.ppermute(own, "c", [(0, 1), (1, 0)])

    core = lax.axis_index("c")
    small = line[:, 0, 240:316]
    partner = lax.ppermute(small, "c", [(0, 1), (1, 0)])
    both = jnp.stack([jnp.where(core == 0, small, partner), jnp.where(core == 0, partner, small)], axis=1)
    steps = both[:, :, 0:15].reshape(MARKERS)
    seen = both[:, :, 16:76].reshape(MARKERS, TGT)
    rates = 1.0 - jnp.exp(-steps.astype(jnp.float32) / map_unit)
    beta = jnp.concatenate([(rates / K) / (1.0 - rates), zero((16,), jnp.float32)])
    keep = jnp.concatenate([1.0 - rates, jnp.ones((16,), jnp.float32)])
    if_one = jnp.where(seen == 2, 1.0, jnp.where(seen == 1, hit, miss)).astype(jnp.float32)
    if_zero = jnp.where(seen == 2, 1.0, jnp.where(seen == 0, hit, miss)).astype(jnp.float32)
    em = jnp.stack([if_one, if_zero], axis=2)
    emv = em.reshape(BLOCKS, 3, TGT, 2).transpose(1, 3, 2, 0).reshape(6, TGT, BLOCKS)
    emv = jnp.pad(emv, ((0, 0), (0, 8 - TGT), (0, LANES - BLOCKS)))
    place = (2 * lax.axis_index("z") + core).astype(jnp.int32).reshape(1)
    return chains(place, beta, keep, em.reshape(MARKERS * 8), own, other,
                  planes(start_weights), planes(end_weights), emv)


def solution(mesh):
    cut = Mesh(mesh.devices.reshape(8, 2, 4, 8), ("z", "c", "x", "y"))
    grp, hap = ("z", "c"), ("x", "y")
    in_specs = (P(grp, hap), P(grp, hap), P(grp), P(hap, None), P(hap, None))
    return jax.shard_map(local, mesh=cut, in_specs=in_specs, out_specs=P(grp, hap), check_vma=False)
```

time: 1190 us -> 76.9 us (0.06)
  starting transfers between devices: 502 us -> 17.1 us
  waiting for transfers between devices: 438 us -> 0.01 us
  local copies, waits for them, and re-layouts: 151 us -> 16.7 us
  other arithmetic: 58.3 us -> 0.16 us
  loops' own time: 36.5 us -> 0 us
  Pallas kernels: 0 us -> 25 us
  blocking collectives: 0 us -> 17.3 us
    ppermute x32 -> x2, starting transfers between devices: 492 us -> 7.47 us  [the longest x1 4.29 us: local(): partner = lax.ppermute(small, 'c', [(0, 1), (1, 0)])]
    ppermute x32 -> x2, waiting for transfers between devices: 433 us -> 0.01 us  [the longest x1 0.01 us: local(): partner = lax.ppermute(small, 'c', [(0, 1), (1, 0)])]
    shift_right_arithmetic x37 -> x0, local copies, waits for them, and re-layouts: 125 us -> none  [unpack_alleles(): jnp.right_shift(packed[:, :, None], shifts[None, None, :])]
    another operation x35 -> x0, loops' own time: 36.5 us -> none  [the longest x1 17.6 us: backward_pass(): return lax.scan(retreat, state, (haplos, observed, rates), reverse=True)]
    pallas_call x0 -> x1, Pallas kernels: none -> 25 us  [chains(): pl.pallas_call(kernel, out_shape=jax.ShapeDtypeStruct((SPAN, TGT), f32),...]
    dynamic_update_slice x30 -> x0, other arithmetic: 22.4 us -> none  [forward_pass(): return lax.scan(advance, state, (haplos, observed, rates))]
    reduce_sum x62 -> x0, other arithmetic: 21.8 us -> none  [the longest x15 5.88 us: advance(): weighted = weighted / jnp.sum(weighted, axis=1, keepdims=True)]
    dynamic_slice x30 -> x0, local copies, waits for them, and re-layouts: 17.3 us -> none  [forward_pass(): return lax.scan(advance, state, (haplos, observed, rates))]
  transfers between devices with their start and end apart: 33 -> 3, of which waited for: 30 -> 0; matrix products, arithmetic and copies ran while one was open for 3% -> 17% of each run, Pallas kernels for 0% -> 0%
where the time goes in v1:
time: 76.9 us; the launch traced here: 76.5 us
  Pallas kernels  25 us (33%)
  blocking collectives  17.3 us (22%)
  starting transfers between devices  17.1 us (22%)
  local copies, waits for them, and re-layouts  16.7 us (22%)
    pallas_call x1, Pallas kernels, chains(): pl.pallas_call(kernel, out_shape=jax.ShapeDtypeStruct((SPAN, TGT), f32),...  25 us
    all_to_all x1, blocking collectives, to_all(): lax.all_to_all(jnp.broadcast_to(array[None], (peers, *array.shape)), axes...  17.3 us
    all_to_all x1, starting transfers between devices, to_all(): lax.all_to_all(jnp.broadcast_to(array[None], (peers, *array.shape)), axes...  9.67 us
    reshape x2, local copies, waits for them, and re-layouts, planes(): split = weights.reshape(TGT, 4, LANES, 2, 15)  7.77 us
    ppermute x1, starting transfers between devices, local(): partner = lax.ppermute(small, 'c', [(0, 1), (1, 0)])  4.29 us
    ppermute x1, starting transfers between devices, local(): other = lax.ppermute(own, 'c', [(0, 1), (1, 0)])  3.19 us
    transpose x2, local copies, waits for them, and re-layouts, planes(): return split.transpose(0, 4, 3, 1, 2).reshape(TGT, TILES, 8, LANES)  1.95 us
    another operation x1, local copies, waits for them, and re-layouts, local(): em = jnp.stack([if_one, if_zero], axis=2)  1.57 us
  transfers between devices with their start and end apart: 3, of which 0 were waited for; matrix products, arithmetic and copies ran while one was open for 17% of the time, Pallas kernels for 0%

profile of v1, /device:TPU:1, one launch (start us, length us, event | category | flops | bytes accessed | tf_op | source)
XLA Modules:
  0.0 76.5 jit_solution(1635653367763397962)
XLA Ops:
  0.0 0.8 %reshape.170 = s32[1,240]{1,0:T(1,128)S(1)} reshape(s32[15,16]{1,0:T(8,128)} %param.5) | data formatting | bytes 1920 | tf_op jit(solution)/shard_map/reshape | solution.py:297
  0.8 0.8 %copy.46 = s32[15,4]{1,0:T(8,128)S(1)} copy(s32[15,4]{0,1:T(4,128)} %param.6) | data formatting | bytes 480 | tf_op args[1]
  1.5 0.1 reshape.172
  1.6 0.7 concatenate.10
  2.4 17.3 %all_to_all.10 = s32[8,1,384]{2,1,0:T(1,128)S(1)} all-to-all(s32[8,1,384]{2,1,0:T(1,128)S(1)} %broadcast_in_dim.35), channel_id=1, replica_groups=mesh['z'=8,'c'=2,'x'=4,'y'=8] {'z'}, dimensions={0} | all-to-all | bytes 24576 | tf_op jit(solution)/shard_map/all_to_all | solution.py:286
  19.7 0.9 %broadcast_in_dim.40 = s32[32,1,3072]{2,1,0:T(1,128)} broadcast(s32[3072]{0:T(1024)S(1)} %bitcast.22), dimensions={2} | broadcast | bytes 405504 | tf_op jit(solution)/shard_map/broadcast_in_dim | solution.py:286
  20.6 9.7 %all-to-all-start.1 = ((s32[32,1,3072]{2,1,0:T(1,128)}), s32[32,1,3072]{2,1,0:T(1,128)S(1)}, u32[]{:S(2)}, u32[]{:S(2)}) async-start(s32[32,1,3072]{2,1,0:T(1,128)} %broadcast_in_dim.40), calls=%async_computation.1 | async-start | bytes 786432 | tf_op jit(solution)/shard_map/all_to_all | solution.py:286
  30.3 0.1 slice.12
  30.4 4.3 %collective-permute-start = (s32[8,76]{1,0:T(8,128)S(1)}, s32[8,76]{1,0:T(8,128)S(1)}, u32[]{:S(2)}, u32[]{:S(2)}) collective-permute-start(s32[8,76]{1,0:T(8,128)S(1)} %bitcast.24), channel_id=1, source_target_pairs={{0,32},{32,0},{1,33},{33,1},{2,34},{34,2},{3,35},{35,3},{4,36},{36... | collective-permute-start | bytes 7304 | tf_op jit(solution)/shard_map/ppermute | solution.py:306
  34.7 0.0 copy-start
  34.7 4.4 %reshape.175 = f32[4,4,128,2,15]{4,3,2,1,0:T(2,128)S(1)} reshape(f32[4,15360]{1,0:T(4,128)} %param.8) | data formatting | bytes 491520 | tf_op jit(solution)/shard_map/reshape | solution.py:290
  39.1 1.0 %copy.52 = f32[4,15,2,4,128]{4,3,2,1,0:T(4,128)S(1)} copy(f32[4,15,2,4,128]{1,2,4,3,0:T(2,128)S(1)} %bitcast.20) | data formatting | bytes 491520 | tf_op jit(solution)/shard_map/transpose | solution.py:291
  40.1 0.0 copy-done
  40.1 3.4 %reshape.177 = f32[4,4,128,2,15]{4,3,2,1,0:T(2,128)S(1)} reshape(f32[4,15360]{1,0:T(4,128)S(1)} %copy-done) | data formatting | bytes 491520 | tf_op jit(solution)/shard_map/reshape | solution.py:290
  43.5 1.0 %copy.53 = f32[4,15,2,4,128]{4,3,2,1,0:T(4,128)S(1)} copy(f32[4,15,2,4,128]{1,2,4,3,0:T(2,128)S(1)} %bitcast.21) | data formatting | bytes 491520 | tf_op jit(solution)/shard_map/transpose | solution.py:291
  44.5 0.0 collective-permute-done
  44.5 0.0 all-to-all-done.1
  44.5 3.2 %collective-permute-start.1 = (s32[768,128]{1,0:T(8,128)S(1)}, s32[768,128]{1,0:T(8,128)S(1)}, u32[]{:S(2)}, u32[]{:S(2)}) collective-permute-start(s32[768,128]{1,0:T(8,128)S(1)} %bitcast.16), channel_id=1, source_target_pairs={{0,32},{32,0},{1,33},{33,1},{2,34},{34,2},{3,35},{35,3},{4,36},{36... | collective-permute-start | bytes 1179656 | tf_op jit(solution)/shard_map/ppermute | solution.py:302
  47.7 0.1 select_select_fusion.1
  47.8 0.1 select_n.106
  47.9 0.1 select_n.108
  48.1 0.1 select_n.103
  48.2 0.1 select_n.107
  48.3 0.1 reshape.183
  48.4 0.1 reshape.185
  48.6 1.6 %copy.51 = f32[240,4,2]{2,1,0:T(4,128)S(1)} copy(f32[240,4,2]{1,0,2:T(8,128)S(1)} %pad_maximum_fusion) | data formatting | bytes 15360 | tf_op jit(solution)/shard_map/stack | solution.py:315
  50.2 0.4 reshape.173.em
  50.6 0.1 copy.57
  50.7 0.1 copy.56
  50.9 0.0 collective-permute-done.1.other
  50.9 25.0 %shard_map.55 = f32[15,4]{1,0:T(8,128)S(1)} custom-call(s32[1]{0:T(128)} %bitcast.place, f32[256]{0:T(256)S(1)} %concatenate.11.beta, f32[256]{0:T(256)S(1)} %concatenate.12.keep, f32[1920]{0:T(1024)S(1)} %reshape.173.em, s32[768,128]{1,0:T(8,128)S(1)} %bitcast.17, s32[768,128]{1,0:T(8,128)S(1)} %collective-permute-done.1.other, ...), custom_call_target="tpu_custom_call" | custom-call | tf_op jit(solution)/shard_map/pallas_call | solution.py:260
  75.8 0.7 copy.58
  (15 shorter events, 0.1 us)
Async XLA Ops:
  20.6 23.9 %all-to-all-start.1 = ((s32[32,1,3072]{2,1,0:T(1,128)}), s32[32,1,3072]{2,1,0:T(1,128)S(1)}, u32[]{:S(2)}, u32[]{:S(2)}) async-start(s32[32,1,3072]{2,1,0:T(1,128)} %broadcast_in_dim.40), calls=%async_computation.1 | async-start | bytes 786432 | tf_op jit(solution)/shard_map/all_to_all | solution.py:286
  30.4 14.1 %collective-permute-start = (s32[8,76]{1,0:T(8,128)S(1)}, s32[8,76]{1,0:T(8,128)S(1)}, u32[]{:S(2)}, u32[]{:S(2)}) collective-permute-start(s32[8,76]{1,0:T(8,128)S(1)} %bitcast.24), channel_id=1, source_target_pairs={{0,32},{32,0},{1,33},{33,1},{2,34},{34,2},{3,35},{35,3},{4,36},{36... | collective-permute-start | bytes 7304 | tf_op jit(solution)/shard_map/ppermute | solution.py:306
  34.7 5.4 %copy-start = (f32[4,15360]{1,0:T(4,128)S(1)}, f32[4,15360]{1,0:T(4,128)}, u32[]{:S(2)}) copy-start(f32[4,15360]{1,0:T(4,128)} %param.9) | copy-start | bytes 737284
  44.5 6.4 %collective-permute-start.1 = (s32[768,128]{1,0:T(8,128)S(1)}, s32[768,128]{1,0:T(8,128)S(1)}, u32[]{:S(2)}, u32[]{:S(2)}) collective-permute-start(s32[768,128]{1,0:T(8,128)S(1)} %bitcast.16), channel_id=1, source_target_pairs={{0,32},{32,0},{1,33},{33,1},{2,34},{34,2},{3,35},{35,3},{4,36},{36... | collective-permute-start | bytes 1179656 | tf_op jit(solution)/shard_map/ppermute | solution.py:302

commit v2 on v1

v2 whole, which is shorter than its diff:
```python
import jax
import jax.numpy as jnp
from jax import lax
from jax.experimental import pallas as pl
from jax.experimental.pallas import tpu as pltpu
from jax.sharding import Mesh, PartitionSpec as P

K = 15360
MARKERS = 240
GROUPS = 16
SPAN = 15
TILES = 15
TGT = 4
BLOCKS = MARKERS // 3
LANES = 128
CHUNK = 1920
hit = 0.99
miss = 0.01
map_unit = 100000.0
lift = float(2**60)


def full(value):
    return jnp.broadcast_to(value, (8, LANES))


def total(tile):
    rows = jnp.sum(tile, axis=0, keepdims=True)
    return full(jnp.sum(rows, axis=1, keepdims=True))


def swapped_blocks(tiles, lane):
    tiles = list(tiles)
    for step in (1, 2, 4):
        low = (lane & (16 * step)) == 0
        for j in range(8):
            if j & step:
                continue
            first, second = tiles[j], tiles[j + step]
            tiles[j] = jnp.where(low, first, pltpu.roll(second, 16 * step, 1))
            tiles[j + step] = jnp.where(low, pltpu.roll(first, LANES - 16 * step, 1), second)
    return tiles


def pack_kernel(alleles, observed, steps, message):
    rows = [alleles[m:m + 1, :] for m in range(SPAN)]
    zero = lambda n: jnp.zeros((1, n), jnp.int32)
    first = jnp.concatenate(rows[:8], axis=1)
    second = jnp.concatenate(rows[8:] + [zero(16)], axis=1)
    seen = [observed[t:t + 1, :] for t in range(TGT)]
    third = jnp.concatenate([steps[...], zero(1)] + seen + [zero(52)], axis=1)
    message[...] = jnp.concatenate([first, second, third] * 8, axis=0)


def pack(alleles, observed, steps):
    vmem = pl.BlockSpec(memory_space=pltpu.VMEM)
    return pl.pallas_call(
        pack_kernel, out_shape=jax.ShapeDtypeStruct((24, LANES), jnp.int32),
        in_specs=[vmem] * 3, out_specs=vmem)(alleles, observed, steps)


def planes_kernel(weights_start, weights_end, start, end, stage, tiles):
    lane = lax.broadcasted_iota(jnp.int32, (8, LANES), 1)
    pair_of = []
    for u in range(TILES):
        offset = (LANES * u) % 30 + lane
        pair_of.append(lax.shift_right_logical(offset - 30 * lax.shift_right_logical(offset * 2185, 16), 1))
    for which, weights in enumerate((weights_start, weights_end)):
        for u in range(TILES):
            for s in range(8):
                at = CHUNK * s + LANES * u
                stage[u, 4 * s:4 * s + 4, :] = weights[:, at:at + LANES]
            for t in range(TGT):
                tiles[which * TGT + t, u] = stage[u, pl.ds(t, 8, stride=4), :]
    for p in range(TILES):
        masks = [pair_of[u] == p for u in range(1, TILES)]
        for row in range(2 * TGT):
            chosen = tiles[row, 0]
            for u in range(1, TILES):
                chosen = jnp.where(masks[u - 1], tiles[row, u], chosen)
            if p:
                chosen = pltpu.roll(chosen, LANES - 2 * p, 1)
            if row < TGT:
                start[row, p] = chosen
            else:
                end[row - TGT, p] = chosen


def planes(weights_start, weights_end):
    vmem = pl.BlockSpec(memory_space=pltpu.VMEM)
    laid = jax.ShapeDtypeStruct((TGT, TILES, 8, LANES), jnp.float32)
    return pl.pallas_call(
        planes_kernel,
        out_shape=(laid, laid),
        in_specs=[vmem] * 2, out_specs=(vmem,) * 2,
        scratch_shapes=[pltpu.VMEM((TILES, 32, LANES), jnp.float32), pltpu.VMEM((2 * TGT, TILES, 8, LANES), jnp.float32)],
        cost_estimate=pl.CostEstimate(flops=4_000_000, transcendentals=0, bytes_accessed=1_000_000),
    )(weights_start, weights_end)


def home_of(group):
    return lax.shift_right_logical(group, 1) + 8 * (group & 1)


def emissions_by_block(sides):
    found = []
    values = sides.astype(jnp.float32).astype(jnp.bfloat16)
    block = lax.broadcasted_iota(jnp.int32, (1, LANES), 1)
    group = lax.shift_right_logical(block * 13108, 16)
    within = block - 5 * group
    home = lax.shift_right_logical(group, 1) + 8 * (group & 1)
    mine = lax.broadcasted_iota(jnp.int32, (16, LANES), 0) == home
    source = lax.broadcasted_iota(jnp.int32, (LANES, LANES), 0)
    for q in range(3):
        rows = []
        for t in range(TGT):
            pick = (source == 16 + 15 * t + 3 * within + q).astype(jnp.float32).astype(jnp.bfloat16)
            moved = jnp.dot(values, pick, preferred_element_type=jnp.float32)
            rows.append(jnp.sum(jnp.where(mine, moved, 0.0), axis=0, keepdims=True))
        seen = jnp.concatenate(rows + rows, axis=0)
        found.append(jnp.where(seen == 2.0, 1.0, jnp.where(seen == 1.0, hit, miss)))
        found.append(jnp.where(seen == 2.0, 1.0, jnp.where(seen == 0.0, hit, miss)))
    return found


def kernel(place, beta, keep, for_one, for_zero, sides, own, other, weights_start, weights_end, out,
           words, fwd, bwd, fstore, bstore, counts_in, sums, gv, gs, nd, eb, sem, weight_sems):
    loads = [pltpu.make_async_copy(weights_start, fwd, weight_sems.at[0]),
             pltpu.make_async_copy(weights_end, bwd, weight_sems.at[1])]
    for load in loads:
        load.start()
    group = place[0]
    core = lax.rem(group, 2)
    lane = lax.broadcasted_iota(jnp.int32, (8, LANES), 1)
    half_lane = lax.shift_right_logical(lane, 1)
    odd = lane & 1
    word_at = (47 * half_lane) & 63

    def unpack(z, carry):
        for ref, which in ((own, core), (other, 1 - core)):
            tiles = [ref[pl.ds(16 * q + 2 * z + a, 8, stride=64), :] for a in range(2) for q in range(4)]
            tiles = swapped_blocks(tiles, lane)
            first = (2 * z + which) * SPAN
            for m in range(SPAN):
                picked = jnp.take_along_axis(tiles[m % 8], word_at + (64 if m >= 8 else 0), axis=1)
                words[first + m] = lax.shift_right_logical(picked, odd)
        return carry

    lax.fori_loop(0, 8, unpack, 0, unroll=4)

    def emission(row, m, t):
        at = 16 + 15 * t + m
        return for_one[row, at], for_zero[row, at]

    def count(block, carry):
        w0, w1, w2 = [words[3 * block + j] & 0x15555555 for j in range(3)]
        w01, w12, w02 = w0 & w1, w1 & w2, w0 & w2
        for q, w in enumerate((w0, w1, w2, w01, w12, w02, w01 & w2)):
            ones = lax.population_count(w).astype(jnp.float32)
            counts_in[q, pl.ds(block, 1), :] = jnp.sum(ones, axis=0, keepdims=True)
        return carry

    lax.fori_loop(0, BLOCKS, count, 0, unroll=4)
    ones = jnp.ones((8, LANES), jnp.bfloat16)
    n = []
    for q in range(7):
        table = counts_in[q].astype(jnp.bfloat16)
        n.append(lax.dot_general(ones, table, (((1,), (1,)), ((), ())), preferred_element_type=jnp.float32))
    n0, n1, n2, n01, n12, n02, n012 = n
    a1, a0, b1, b0, c1, c0 = emissions_by_block(sides[...])

    def pair(x1, x0, y1, y0, nx, ny, nxy):
        return nxy * (x1 * y1) + (nx - nxy) * (x1 * y0) + (ny - nxy) * (x0 * y1) + (K - nx - ny + nxy) * (x0 * y0)

    table0 = n0 * a1 + (K - n0) * a0
    table1 = n1 * b1 + (K - n1) * b0
    table2 = n2 * c1 + (K - n2) * c0
    table3 = pair(a1, a0, b1, b0, n0, n1, n01)
    table4 = pair(b1, b0, c1, c0, n1, n2, n12)
    with_a = n012 * (b1 * c1) + (n01 - n012) * (b1 * c0) + (n02 - n012) * (b0 * c1) + (n0 - n01 - n02 + n012) * (b0 * c0)
    rest = (n12 - n012) * (b1 * c1) + (n1 - n01 - n12 + n012) * (b1 * c0) + (n2 - n02 - n12 + n012) * (b0 * c1) \
        + (K - n0 - n1 - n2 + n01 + n12 + n02 - n012) * (b0 * c0)
    table5 = a1 * with_a + a0 * rest
    for i, table in enumerate((table0, table1, table2, table3, table4, table5)):
        gv[TGT * i:TGT * i + TGT, :] = table[0:TGT]
    copy = pltpu.make_async_copy(gv, gs, sem)
    copy.start()

    for load in loads:
        load.wait()

    def sum_of(ref):
        sums_now = []
        for t in range(TGT):
            acc = ref[t, 0]
            for v in range(1, TILES):
                acc = acc + ref[t, v]
            sums_now.append(total(acc))
        return tuple(sums_now)

    def three(state, block, carry, reverse):
        order = (2, 1, 0) if reverse else (0, 1, 2)
        step = block - 5 * lax.shift_right_logical(block * 13108, 16)
        at = lax.shift_right_logical(block * 13108, 16)
        row = home_of(at)
        tile_words = [words[3 * block + j] for j in order]
        if reverse:
            last = step == 4
            after = jnp.where(last, home_of(jnp.minimum(at + 1, GROUPS - 1)), row)
            edge = beta[after, jnp.where(last, 0, 3 * step + 3)]
            edge = jnp.where(block == BLOCKS - 1, 0.0, edge)
            rates = [edge, beta[row, 3 * step + 2], beta[row, 3 * step + 1]]
        else:
            rates = [beta[row, 3 * step + j] for j in range(3)]
        singles = order
        pairs = (4, 3) if reverse else (3, 4)
        result = [None] * TGT
        new_scale = [jnp.ones((8, LANES), jnp.float32)] * TGT
        sums_of = {}
        emis = {t: [emission(row, 3 * step + j, t) for j in order] for t in range(TGT)}

        def down(targets):
            accs = {t: [None] * 3 for t in targets}
            first = {t: (emis[t][0][0] * carry[4 + t], emis[t][0][1] * carry[4 + t]) for t in targets}
            for v in range(TILES):
                masks = [(w & (1 << (2 * v))) != 0 for w in tile_words]
                for t in targets:
                    y = state[t, v]
                    for j in range(3):
                        e1, e0 = first[t] if j == 0 else emis[t][j]
                        e = jnp.where(masks[j], e1, e0)
                        if j:
                            eb[j - 1, t, v] = e
                        y = y * e
                        accs[t][j] = y if v == 0 else accs[t][j] + y
                    state[t, v] = y
            for t in targets:
                sums_of[t] = [total(a) for a in accs[t]]

        def up(targets):
            mix = {}
            for t in targets:
                q1, q2, q3 = sums_of[t]
                g = lambda q: gs[TGT * q + t, block]
                m0 = rates[0] * (carry[t] * carry[4 + t])
                s1 = q1 + m0 * g(singles[0])
                m1 = rates[1] * s1
                s2 = (q2 + m0 * g(pairs[0])) + m1 * g(singles[1])
                m2 = rates[2] * s2
                s3 = (q3 + m0 * g(5)) + m1 * g(pairs[1]) + m2 * g(singles[2])
                result[t] = s3
                mix[t] = (m0 * emis[t][0][0] + m1, m0 * emis[t][0][1] + m1, m2)
            for v in range(TILES):
                mask = (tile_words[0] & (1 << (2 * v))) != 0
                for t in targets:
                    h = jnp.where(mask, mix[t][0], mix[t][1])
                    h = h * eb[0, t, v] + mix[t][2]
                    h = h * eb[1, t, v]
                    state[t, v] = state[t, v] + h

        down((0, 1))
        down((2, 3))
        up((0, 1))
        up((2, 3))
        return tuple(result) + tuple(new_scale)

    start_sums, end_sums = sum_of(fwd), sum_of(bwd)
    copy.wait()

    def run(state, first, count_groups, reverse, sums_now):
        def one_group(i, sums_now):
            block = (first - i if reverse else first + i) * 5
            carry = tuple(sums_now) + tuple(lift / s for s in sums_now)
            def one_block(j, carry):
                return three(state, block + (4 - j if reverse else j), carry, reverse)
            return lax.fori_loop(0, 5, one_block, carry, unroll=5)[:TGT]
        return lax.fori_loop(0, count_groups, one_group, sums_now)

    fsum = run(fwd, 0, group, False, start_sums)
    bsum = run(bwd, GROUPS - 1, GROUPS - 1 - group, True, end_sums)

    begin = group * SPAN
    here = home_of(group)
    after = home_of(jnp.minimum(group + 1, GROUPS - 1))

    def later(m):
        last = m == SPAN - 1
        return jnp.where(last, after, here), jnp.where(last, 0, m + 1), jnp.logical_and(last, group == GROUPS - 1)

    scale_f = tuple(lift / s for s in fsum)
    scale_b = tuple(lift / s for s in bsum)

    def own_step(i, carry):
        fs, bs, ff, bf = carry[0:4], carry[4:8], carry[8:12], carry[12:16]
        up_to = SPAN - 1 - i
        wf, wb = words[begin + i], words[begin + up_to]
        row, at, none = later(up_to)
        rate_b = jnp.where(none, 0.0, beta[row, at])
        fnew, bnew = [], []
        for t in range(TGT):
            mix = beta[here, i] * fs[t]
            e1, e0 = emission(here, i, t)
            e1, e0 = e1 * ff[t], e0 * ff[t]
            acc = None
            for v in range(TILES):
                x = (fwd[t, v] + mix) * jnp.where((wf & (1 << (2 * v))) != 0, e1, e0)
                fwd[t, v] = x
                fstore[i * TGT + t, v] = x
                acc = x if v == 0 else acc + x
            fnew.append(acc)
        for t in range(TGT):
            mix = rate_b * bs[t]
            e1, e0 = emission(here, up_to, t)
            e1, e0 = e1 * bf[t], e0 * bf[t]
            sums[1, (SPAN - 1 - i) * TGT + t] = bs[t]
            acc = None
            for v in range(TILES):
                b = bwd[t, v] + mix
                bstore[(SPAN - 1 - i) * TGT + t, v] = b
                x = b * jnp.where((wb & (1 << (2 * v))) != 0, e1, e0)
                bwd[t, v] = x
                acc = x if v == 0 else acc + x
            bnew.append(acc)
        fnew = [total(a) for a in fnew]
        bnew = [total(a) for a in bnew]
        for t in range(TGT):
            sums[0, i * TGT + t] = fnew[t]
        one = jnp.ones((8, LANES), jnp.float32)
        return tuple(fnew) + tuple(bnew) + (one,) * 8

    lax.fori_loop(0, SPAN, own_step, tuple(fsum) + tuple(bsum) + scale_f + scale_b, unroll=3)

    def dose(i, carry):
        w = words[begin + i]
        at_row, at, none = later(i)
        kept = jnp.where(none, 1.0, keep[at_row, at])
        for t in range(TGT):
            row = i * TGT + t
            by_f = 1.0 / sums[0, row]
            by_b = kept / sums[1, row]
            num = den = None
            for v in range(TILES):
                f = (fstore[row, v] * by_f).astype(jnp.bfloat16).astype(jnp.float32)
                b = (bstore[row, v] * by_b).astype(jnp.bfloat16).astype(jnp.float32)
                p = f * b
                q = jnp.where((w & (1 << (2 * v))) != 0, p, 0.0)
                num = q if v == 0 else num + q
                den = p if v == 0 else den + p
            nd[0, t, pl.ds(i, 1), :] = jnp.sum(num, axis=0, keepdims=True)
            nd[1, t, pl.ds(i, 1), :] = jnp.sum(den, axis=0, keepdims=True)
        return carry

    lax.fori_loop(0, SPAN, dose, 0, unroll=3)
    line = jnp.ones((8, LANES), jnp.float32)
    which = lax.broadcasted_iota(jnp.int32, (8, 16), 0)
    answer = jnp.zeros((8, 16), jnp.float32)
    for t in range(TGT):
        num, den = [
            lax.dot_general(line, nd[i, t], (((1,), (1,)), ((), ())), precision=lax.Precision.HIGHEST,
                            preferred_element_type=jnp.float32) for i in range(2)]
        answer = jnp.where(which == t, num / den, answer)
    out[...] = answer[0:TGT, 0:SPAN]


def chains(place, beta, keep, for_one, for_zero, sides, own, other, weights_start, weights_end):
    smem = pl.BlockSpec(memory_space=pltpu.SMEM)
    vmem = pl.BlockSpec(memory_space=pltpu.VMEM)
    f32 = jnp.float32
    return pl.pallas_call(
        kernel,
        out_shape=jax.ShapeDtypeStruct((TGT, SPAN), f32),
        in_specs=[smem] * 5 + [vmem] * 3 + [pl.BlockSpec(memory_space=pl.ANY)] * 2,
        out_specs=vmem,
        scratch_shapes=[
            pltpu.VMEM((MARKERS, 8, LANES), jnp.int32),
            pltpu.VMEM((TGT, TILES, 8, LANES), f32),
            pltpu.VMEM((TGT, TILES, 8, LANES), f32),
            pltpu.VMEM((SPAN * TGT, TILES, 8, LANES), f32),
            pltpu.VMEM((SPAN * TGT, TILES, 8, LANES), f32),
            pltpu.VMEM((7, LANES, LANES), f32),
            pltpu.VMEM((2, SPAN * TGT, 8, LANES), f32),
            pltpu.VMEM((24, LANES), f32),
            pltpu.SMEM((24, LANES), f32),
            pltpu.VMEM((2, TGT, 16, LANES), f32),
            pltpu.VMEM((2, TGT, TILES, 8, LANES), f32),
            pltpu.SemaphoreType.DMA,
            pltpu.SemaphoreType.DMA((2,)),
        ],
        compiler_params=pltpu.CompilerParams(vmem_limit_bytes=60 << 20),
    )(place, beta, keep, for_one, for_zero, sides, own, other, weights_start, weights_end)


def local(alleles, observed, map_steps, start_weights, end_weights):
    message = pack(alleles, observed.T, map_steps.reshape(1, SPAN)).reshape(8, 1, 384)
    start, end = planes(start_weights, end_weights)
    line = lax.all_to_all(message, "z", 0, 0, tiled=True)
    spread = jnp.broadcast_to(line[:, :, 0:256].reshape(1, 1, 2048), (32, 1, 2048))
    own = lax.all_to_all(spread, ("x", "y"), 0, 0, tiled=True).reshape(512, LANES)
    side = line[:, 0, 256:384]
    swap = [(0, 1), (1, 0)]
    other = lax.ppermute(own, "c", swap)
    partner = lax.ppermute(side, "c", swap)

    core = lax.axis_index("c")
    sides = jnp.concatenate([jnp.where(core == 0, side, partner), jnp.where(core == 0, partner, side)], axis=0)
    rates = 1.0 - jnp.exp(-sides.astype(jnp.float32) / map_unit)
    keep = 1.0 - rates
    beta = (rates / K) / keep
    for_one = jnp.where(sides == 2, 1.0, jnp.where(sides == 1, hit, miss)).astype(jnp.float32)
    for_zero = jnp.where(sides == 2, 1.0, jnp.where(sides == 0, hit, miss)).astype(jnp.float32)
    place = (2 * lax.axis_index("z") + core).astype(jnp.int32).reshape(1)
    return chains(place, beta, keep, for_one, for_zero, sides, own, other, start, end).T


def solution(mesh):
    cut = Mesh(mesh.devices.reshape(8, 2, 4, 8), ("z", "c", "x", "y"))
    grp, hap = ("z", "c"), ("x", "y")
    in_specs = (P(grp, hap), P(grp, hap), P(grp), P(hap, None), P(hap, None))
    return jax.shard_map(local, mesh=cut, in_specs=in_specs, out_specs=P(grp, hap), check_vma=False)
```

time: 76.9 us -> 70.5 us (0.917)
  local copies, waits for them, and re-layouts: 16.7 us -> 1.55 us
  waiting for transfers between devices: 0.01 us -> 3.03 us
  starting transfers between devices: 17.1 us -> 19.9 us
  Pallas kernels: 25 us -> 26.9 us
  other arithmetic: 0.16 us -> 1.22 us
    reshape x5 -> x0, local copies, waits for them, and re-layouts: 9.06 us -> none  [the longest x2 7.77 us: planes(): split = weights.reshape(TGT, 4, LANES, 2, 15)]
    all_to_all x1, waiting for transfers between devices: 0.01 us -> 3.03 us  [local(): lax.all_to_all(spread, ('x', 'y'), 0, 0, tiled=True).reshape(512, LANES)]
    ppermute x2, starting transfers between devices: 7.47 us -> 10.3 us  [the longest x1 5.96 us: local(): other = lax.ppermute(own, 'c', swap)]
    transpose x2 -> x0, local copies, waits for them, and re-layouts: 1.95 us -> none  [planes(): return split.transpose(0, 4, 3, 1, 2).reshape(TGT, TILES, 8, LANES)]
    pallas_call x1 -> x3, Pallas kernels: 25 us -> 26.9 us  [the longest x1 23.2 us: chains(): pl.pallas_call(kernel, out_shape=jax.ShapeDtypeStruct((TGT, SPAN), f32),...]
    another operation x1 -> x0, local copies, waits for them, and re-layouts: 1.57 us -> none  [local(): em = jnp.stack([if_one, if_zero], axis=2)]
  transfers between devices with their start and end apart: 3 -> 3, of which waited for: 0 -> 1; matrix products, arithmetic and copies ran while one was open for 17% -> 2% of each run, Pallas kernels for 0% -> 3%
where the time goes in v2:
time: 70.5 us; the launch traced here: 70.1 us
  Pallas kernels  26.9 us (38%)
  starting transfers between devices  19.9 us (28%)
  blocking collectives  17.5 us (25%)
  waiting for transfers between devices  3.03 us (4%)
  local copies, waits for them, and re-layouts  1.55 us (2%)
  other arithmetic  1.22 us (2%)
    pallas_call x1, Pallas kernels, chains(): pl.pallas_call(kernel, out_shape=jax.ShapeDtypeStruct((TGT, SPAN), f32),...  23.2 us
    all_to_all x1, blocking collectives, local(): line = lax.all_to_all(message, 'z', 0, 0, tiled=True)  17.5 us
    all_to_all x1, starting transfers between devices, local(): lax.all_to_all(spread, ('x', 'y'), 0, 0, tiled=True).reshape(512, LANES)  9.67 us
    ppermute x1, starting transfers between devices, local(): other = lax.ppermute(own, 'c', swap)  5.96 us
    ppermute x1, starting transfers between devices, local(): partner = lax.ppermute(side, 'c', swap)  4.29 us
    all_to_all x1, waiting for transfers between devices, local(): lax.all_to_all(spread, ('x', 'y'), 0, 0, tiled=True).reshape(512, LANES)  3.03 us
    pallas_call x1, Pallas kernels, planes(): pl.pallas_call(planes_kernel, out_shape=(laid, laid), in_specs=[vmem] * 2...  2.3 us
  transfers between devices with their start and end apart: 3, of which 1 were waited for; matrix products, arithmetic and copies ran while one was open for 2% of the time, Pallas kernels for 3%

profile of v2, /device:TPU:1, one launch (start us, length us, event | category | flops | bytes accessed | tf_op | source)
XLA Modules:
  0.0 70.1 jit_solution(16031223697602804960)
XLA Ops:
  0.0 1.4 %shard_map.55 = s32[24,128]{1,0:T(8,128)} custom-call(s32[15,16]{1,0:T(8,128)} %alleles.1, s32[4,15]{1,0:T(4,128)} %bitcast.16, s32[1,15]{1,0:T(1,128)} %bitcast.17), custom_call_target="tpu_custom_call" | custom-call | tf_op jit(solution)/shard_map/pallas_call | solution.py:57
  1.4 17.5 %all_to_all.10 = s32[8,1,384]{2,1,0:T(1,128)S(1)} all-to-all(s32[8,1,384]{2,1,0:T(1,128)} %bitcast.12), channel_id=1, replica_groups=mesh['z'=8,'c'=2,'x'=4,'y'=8] {'z'}, dimensions={0} | all-to-all | bytes 24576 | tf_op jit(solution)/shard_map/all_to_all | solution.py:396
  18.9 0.8 %broadcast_in_dim.23 = s32[32,1,2048]{2,1,0:T(1,128)} broadcast(s32[2048]{0:T(1024)S(1)} %bitcast.13), dimensions={2} | broadcast | bytes 270336 | tf_op jit(solution)/shard_map/broadcast_in_dim | solution.py:397
  19.7 9.7 %all-to-all-start.1 = ((s32[32,1,2048]{2,1,0:T(1,128)}), s32[32,1,2048]{2,1,0:T(1,128)S(1)}, u32[]{:S(2)}, u32[]{:S(2)}) async-start(s32[32,1,2048]{2,1,0:T(1,128)} %broadcast_in_dim.23), calls=%async_computation.1 | async-start | bytes 524288 | tf_op jit(solution)/shard_map/all_to_all | solution.py:398
  29.4 4.3 %collective-permute-start = (s32[8,128]{1,0:T(8,128)S(1)}, s32[8,128]{1,0:T(8,128)S(1)}, u32[]{:S(2)}, u32[]{:S(2)}) collective-permute-start(s32[8,128]{1,0:T(8,128)S(1)} %bitcast.14), channel_id=1, source_target_pairs={{0,32},{32,0},{1,33},{33,1},{2,34},{34,2},{3,35},{35,3},{4,36},{36... | collective-permute-start | bytes 12296 | tf_op jit(solution)/shard_map/ppermute | solution.py:402
  33.7 2.3 %shard_map.56 = (f32[4,15,8,128]{3,2,1,0:T(8,128)}, f32[4,15,8,128]{3,2,1,0:T(8,128)}) custom-call(f32[4,15360]{1,0:T(4,128)} %weights_start.1, f32[4,15360]{1,0:T(4,128)} %weights_end.1), custom_call_target="tpu_custom_call" | custom-call | flops 4000000 | bytes 1000000 | tf_op jit(solution)/shard_map/pallas_call | solution.py:92
  36.0 3.0 %all-to-all-done.1 = s32[32,1,2048]{2,1,0:T(1,128)S(1)} async-done(((s32[32,1,2048]{2,1,0:T(1,128)}), s32[32,1,2048]{2,1,0:T(1,128)S(1)}, u32[]{:S(2)}, u32[]{:S(2)}) %all-to-all-start.1) | async-done | bytes 262176 | tf_op jit(solution)/shard_map/all_to_all | solution.py:398
  39.0 0.0 copy-start
  39.0 6.0 %collective-permute-start.1 = (s32[512,128]{1,0:T(8,128)S(1)}, s32[512,128]{1,0:T(8,128)S(1)}, u32[]{:S(2)}, u32[]{:S(2)}) collective-permute-start(s32[512,128]{1,0:T(8,128)S(1)} %bitcast.10), channel_id=1, source_target_pairs={{0,32},{32,0},{1,33},{33,1},{2,34},{34,2},{3,35},{35,3},{4,36},{36... | collective-permute-start | bytes 786440 | tf_op jit(solution)/shard_map/ppermute | solution.py:401
  45.0 0.0 collective-permute-done
  45.0 0.6 pad_add_fusion.sides
  45.6 0.6 select_select_fusion
  46.2 0.0 collective-permute-done.1.other
  46.2 0.0 copy-start.1
  46.2 0.0 copy-done
  46.3 0.7 %copy-done.1 = s32[512,128]{1,0:T(8,128)} copy-done((s32[512,128]{1,0:T(8,128)}, s32[512,128]{1,0:T(8,128)S(1)}, u32[]{:S(2)}) %copy-start.1) | copy-done | bytes 262168
  47.0 23.2 %shard_map.57 = f32[4,15]{1,0:T(4,128)} custom-call(s32[1]{0:T(128)} %bitcast.place, f32[16,128]{1,0:T(8,128)} %get-tuple-element.10.beta, f32[16,128]{1,0:T(8,128)} %get-tuple-element.11.keep, f32[16,128]{1,0:T(8,128)} %get-tuple-element.12.for_one, f32[16,128]{1,0:T(8,128)} %get-tuple-element.9.for_zero, s32[16,128]{1,0:T(8,128)} %pad_add_fusion.sides, ...), custom_call_target="tpu_custom_call" | custom-call | tf_op jit(solution)/shard_map/pallas_call | solution.py:369
  (3 shorter events, 0.0 us)
Async XLA Ops:
  19.7 19.3 %all-to-all-start.1 = ((s32[32,1,2048]{2,1,0:T(1,128)}), s32[32,1,2048]{2,1,0:T(1,128)S(1)}, u32[]{:S(2)}, u32[]{:S(2)}) async-start(s32[32,1,2048]{2,1,0:T(1,128)} %broadcast_in_dim.23), calls=%async_computation.1 | async-start | bytes 524288 | tf_op jit(solution)/shard_map/all_to_all | solution.py:398
  29.4 15.6 %collective-permute-start = (s32[8,128]{1,0:T(8,128)S(1)}, s32[8,128]{1,0:T(8,128)S(1)}, u32[]{:S(2)}, u32[]{:S(2)}) collective-permute-start(s32[8,128]{1,0:T(8,128)S(1)} %bitcast.14), channel_id=1, source_target_pairs={{0,32},{32,0},{1,33},{33,1},{2,34},{34,2},{3,35},{35,3},{4,36},{36... | collective-permute-start | bytes 12296 | tf_op jit(solution)/shard_map/ppermute | solution.py:402
  39.0 7.2 %copy-start = (s32[32,1,2048]{2,1,0:T(1,128)}, s32[32,1,2048]{2,1,0:T(1,128)S(1)}, u32[]{:S(2)}) copy-start(s32[32,1,2048]{2,1,0:T(1,128)S(1)} %all-to-all-done.1) | copy-start | bytes 786436
  39.0 7.2 %collective-permute-start.1 = (s32[512,128]{1,0:T(8,128)S(1)}, s32[512,128]{1,0:T(8,128)S(1)}, u32[]{:S(2)}, u32[]{:S(2)}) collective-permute-start(s32[512,128]{1,0:T(8,128)S(1)} %bitcast.10), channel_id=1, source_target_pairs={{0,32},{32,0},{1,33},{33,1},{2,34},{34,2},{3,35},{35,3},{4,36},{36... | collective-permute-start | bytes 786440 | tf_op jit(solution)/shard_map/ppermute | solution.py:401
  46.2 0.7 %copy-start.1 = (s32[512,128]{1,0:T(8,128)}, s32[512,128]{1,0:T(8,128)S(1)}, u32[]{:S(2)}) copy-start(s32[512,128]{1,0:T(8,128)S(1)} %collective-permute-done.1.other) | copy-start | bytes 786436

commit v3 on v2

--- a/solution.py
+++ b/solution.py
@@ -146,7 +146,7 @@
                 words[first + m] = lax.shift_right_logical(picked, odd)
         return carry
 
-    lax.fori_loop(0, 8, unpack, 0, unroll=4)
+    lax.fori_loop(0, 8, unpack, 0, unroll=2)
 
     def emission(row, m, t):
         at = 16 + 15 * t + m
@@ -328,7 +328,7 @@
         one = jnp.ones((8, LANES), jnp.float32)
         return tuple(fnew) + tuple(bnew) + (one,) * 8
 
-    lax.fori_loop(0, SPAN, own_step, tuple(fsum) + tuple(bsum) + scale_f + scale_b, unroll=3)
+    lax.fori_loop(0, SPAN, own_step, tuple(fsum) + tuple(bsum) + scale_f + scale_b, unroll=15)
 
     def dose(i, carry):
         w = words[begin + i]
@@ -386,13 +386,13 @@
             pltpu.SemaphoreType.DMA,
             pltpu.SemaphoreType.DMA((2,)),
         ],
-        compiler_params=pltpu.CompilerParams(vmem_limit_bytes=60 << 20),
+        compiler_params=pltpu.CompilerParams(vmem_limit_bytes=40 << 20),
     )(place, beta, keep, for_one, for_zero, sides, own, other, weights_start, weights_end)
 
 
 def local(alleles, observed, map_steps, start_weights, end_weights):
     message = pack(alleles, observed.T, map_steps.reshape(1, SPAN)).reshape(8, 1, 384)
-    start, end = planes(start_weights, end_weights)
+    start, end = [jnp.maximum(x, 0.0) for x in planes(start_weights, end_weights)]
     line = lax.all_to_all(message, "z", 0, 0, tiled=True)
     spread = jnp.broadcast_to(line[:, :, 0:256].reshape(1, 1, 2048), (32, 1, 2048))
     own = lax.all_to_all(spread, ("x", "y"), 0, 0, tiled=True).reshape(512, LANES)

time: 70.5 us -> 69.2 us (0.982)
  local copies, waits for them, and re-layouts: 1.55 us -> 0.84 us
    max x0 -> x1, other arithmetic: none -> 1.1 us  [local(): jnp.maximum(x, 0.0)]
    all_to_all x1, waiting for transfers between devices: 3.03 us -> 1.95 us  [local(): lax.all_to_all(spread, ('x', 'y'), 0, 0, tiled=True).reshape(512, LANES)]
    ppermute x1, waiting for transfers between devices: 0.01 us -> 1.08 us  [local(): other = lax.ppermute(own, 'c', swap)]
    unnamed x4 -> x0, local copies, waits for them, and re-layouts: 0.71 us -> none
  transfers between devices with their start and end apart: 3 -> 3, of which waited for: 1 -> 2; matrix products, arithmetic and copies ran while one was open for 2% -> 2% of each run, Pallas kernels for 3% -> 3%
where the time goes in v3:
time: 69.2 us; the launch traced here: 68.8 us
  Pallas kernels  26.4 us (38%)
  starting transfers between devices  19.9 us (29%)
  blocking collectives  17.5 us (25%)
  waiting for transfers between devices  3.03 us (4%)
  other arithmetic  1.12 us (2%)
  local copies, waits for them, and re-layouts  0.84 us (1%)
    pallas_call x1, Pallas kernels, chains(): pl.pallas_call(kernel, out_shape=jax.ShapeDtypeStruct((TGT, SPAN), f32),...  22.7 us
    all_to_all x1, blocking collectives, local(): line = lax.all_to_all(message, 'z', 0, 0, tiled=True)  17.5 us
    all_to_all x1, starting transfers between devices, local(): lax.all_to_all(spread, ('x', 'y'), 0, 0, tiled=True).reshape(512, LANES)  9.67 us
    ppermute x1, starting transfers between devices, local(): other = lax.ppermute(own, 'c', swap)  5.96 us
    ppermute x1, starting transfers between devices, local(): partner = lax.ppermute(side, 'c', swap)  4.28 us
    pallas_call x1, Pallas kernels, planes(): pl.pallas_call(planes_kernel, out_shape=(laid, laid), in_specs=[vmem] * 2...  2.3 us
    all_to_all x1, waiting for transfers between devices, local(): lax.all_to_all(spread, ('x', 'y'), 0, 0, tiled=True).reshape(512, LANES)  1.95 us
    pallas_call x1, Pallas kernels, pack(): pl.pallas_call(pack_kernel, out_shape=jax.ShapeDtypeStruct((24, LANES), j...  1.4 us
  transfers between devices with their start and end apart: 3, of which 2 were waited for; matrix products, arithmetic and copies ran while one was open for 2% of the time, Pallas kernels for 3%

profile of v3, /device:TPU:1, one launch (start us, length us, event | category | flops | bytes accessed | tf_op | source)
XLA Modules:
  0.0 68.8 jit_solution(15095066610497868838)
XLA Ops:
  0.0 1.4 %shard_map.55 = s32[24,128]{1,0:T(8,128)} custom-call(s32[15,16]{1,0:T(8,128)} %alleles.1, s32[4,15]{1,0:T(4,128)} %bitcast.16, s32[1,15]{1,0:T(1,128)} %bitcast.17), custom_call_target="tpu_custom_call" | custom-call | tf_op jit(solution)/shard_map/pallas_call | solution.py:57
  1.4 17.5 %all_to_all.10 = s32[8,1,384]{2,1,0:T(1,128)S(1)} all-to-all(s32[8,1,384]{2,1,0:T(1,128)} %bitcast.12), channel_id=1, replica_groups=mesh['z'=8,'c'=2,'x'=4,'y'=8] {'z'}, dimensions={0} | all-to-all | bytes 24576 | tf_op jit(solution)/shard_map/all_to_all | solution.py:396
  18.9 0.8 %broadcast_in_dim.23 = s32[32,1,2048]{2,1,0:T(1,128)} broadcast(s32[2048]{0:T(1024)S(1)} %bitcast.13), dimensions={2} | broadcast | bytes 270336 | tf_op jit(solution)/shard_map/broadcast_in_dim | solution.py:397
  19.7 9.7 %all-to-all-start.1 = ((s32[32,1,2048]{2,1,0:T(1,128)}), s32[32,1,2048]{2,1,0:T(1,128)S(1)}, u32[]{:S(2)}, u32[]{:S(2)}) async-start(s32[32,1,2048]{2,1,0:T(1,128)} %broadcast_in_dim.23), calls=%async_computation.1 | async-start | bytes 524288 | tf_op jit(solution)/shard_map/all_to_all | solution.py:398
  29.4 2.3 %shard_map.56 = (f32[4,15,8,128]{3,2,1,0:T(8,128)}, f32[4,15,8,128]{3,2,1,0:T(8,128)}) custom-call(f32[4,15360]{1,0:T(4,128)} %weights_start.1, f32[4,15360]{1,0:T(4,128)} %weights_end.1), custom_call_target="tpu_custom_call" | custom-call | flops 4000000 | bytes 1000000 | tf_op jit(solution)/shard_map/pallas_call | solution.py:92
  31.7 4.3 %collective-permute-start = (s32[8,128]{1,0:T(8,128)S(1)}, s32[8,128]{1,0:T(8,128)S(1)}, u32[]{:S(2)}, u32[]{:S(2)}) collective-permute-start(s32[8,128]{1,0:T(8,128)S(1)} %bitcast.14), channel_id=1, source_target_pairs={{0,32},{32,0},{1,33},{33,1},{2,34},{34,2},{3,35},{35,3},{4,36},{36... | collective-permute-start | bytes 12296 | tf_op jit(solution)/shard_map/ppermute | solution.py:402
  36.0 1.1 %broadcast_maximum_fusion = (f32[4,15,8,128]{3,2,1,0:T(8,128)S(1)}, f32[4,15,8,128]{3,2,1,0:T(8,128)S(1)}) fusion(f32[4,15,8,128]{3,2,1,0:T(8,128)} %get-tuple-element.8, f32[4,15,8,128]{3,2,1,0:T(8,128)} %get-tuple-element.7), kind=kLoop, calls=%fused_computation | loop fusion | flops 122880 | bytes 983040 | tf_op jit(solution)/shard_map/max | solution.py:395
  37.1 1.9 %all-to-all-done.1 = s32[32,1,2048]{2,1,0:T(1,128)S(1)} async-done(((s32[32,1,2048]{2,1,0:T(1,128)}), s32[32,1,2048]{2,1,0:T(1,128)S(1)}, u32[]{:S(2)}, u32[]{:S(2)}) %all-to-all-start.1) | async-done | bytes 262176 | tf_op jit(solution)/shard_map/all_to_all | solution.py:398
  39.0 6.0 %collective-permute-start.1 = (s32[512,128]{1,0:T(8,128)S(1)}, s32[512,128]{1,0:T(8,128)S(1)}, u32[]{:S(2)}, u32[]{:S(2)}) collective-permute-start(s32[512,128]{1,0:T(8,128)S(1)} %bitcast.10), channel_id=1, source_target_pairs={{0,32},{32,0},{1,33},{33,1},{2,34},{34,2},{3,35},{35,3},{4,36},{36... | collective-permute-start | bytes 786440 | tf_op jit(solution)/shard_map/ppermute | solution.py:401
  45.0 0.0 collective-permute-done
  45.1 1.1 %collective-permute-done.1.other = s32[512,128]{1,0:T(8,128)S(1)} collective-permute-done((s32[512,128]{1,0:T(8,128)S(1)}, s32[512,128]{1,0:T(8,128)S(1)}, u32[]{:S(2)}, u32[]{:S(2)}) %collective-permute-start.1) | collective-permute-done | bytes 262176 | tf_op jit(solution)/shard_map/ppermute | solution.py:401
  46.1 22.7 %shard_map.57 = f32[4,15]{1,0:T(4,128)} custom-call(s32[1]{0:T(128)} %bitcast.place, f32[16,128]{1,0:T(8,128)S(1)} %get-tuple-element.10.beta, f32[16,128]{1,0:T(8,128)S(1)} %get-tuple-element.11.keep, f32[16,128]{1,0:T(8,128)S(1)} %get-tuple-element.12.for_one, f32[16,128]{1,0:T(8,128)S(1)} %get-tuple-element.9.for_zero, s32[16,128]{1,0:T(8,128)S(1)} %pad_add_fusion.sides, ...), custom_call_target="tpu_custom_call" | custom-call | tf_op jit(solution)/shard_map/pallas_call | solution.py:369
  (5 shorter events, 0.0 us)
Async XLA Ops:
  19.7 19.3 %all-to-all-start.1 = ((s32[32,1,2048]{2,1,0:T(1,128)}), s32[32,1,2048]{2,1,0:T(1,128)S(1)}, u32[]{:S(2)}, u32[]{:S(2)}) async-start(s32[32,1,2048]{2,1,0:T(1,128)} %broadcast_in_dim.23), calls=%async_computation.1 | async-start | bytes 524288 | tf_op jit(solution)/shard_map/all_to_all | solution.py:398
  31.7 13.3 %collective-permute-start = (s32[8,128]{1,0:T(8,128)S(1)}, s32[8,128]{1,0:T(8,128)S(1)}, u32[]{:S(2)}, u32[]{:S(2)}) collective-permute-start(s32[8,128]{1,0:T(8,128)S(1)} %bitcast.14), channel_id=1, source_target_pairs={{0,32},{32,0},{1,33},{33,1},{2,34},{34,2},{3,35},{35,3},{4,36},{36... | collective-permute-start | bytes 12296 | tf_op jit(solution)/shard_map/ppermute | solution.py:402
  39.0 7.1 %collective-permute-start.1 = (s32[512,128]{1,0:T(8,128)S(1)}, s32[512,128]{1,0:T(8,128)S(1)}, u32[]{:S(2)}, u32[]{:S(2)}) collective-permute-start(s32[512,128]{1,0:T(8,128)S(1)} %bitcast.10), channel_id=1, source_target_pairs={{0,32},{32,0},{1,33},{33,1},{2,34},{34,2},{3,35},{35,3},{4,36},{36... | collective-permute-start | bytes 786440 | tf_op jit(solution)/shard_map/ppermute | solution.py:401

commit v4 on v3

--- a/solution.py
+++ b/solution.py
@@ -160,7 +160,7 @@
             counts_in[q, pl.ds(block, 1), :] = jnp.sum(ones, axis=0, keepdims=True)
         return carry
 
-    lax.fori_loop(0, BLOCKS, count, 0, unroll=4)
+    lax.fori_loop(0, BLOCKS, count, 0, unroll=8)
     ones = jnp.ones((8, LANES), jnp.bfloat16)
     n = []
     for q in range(7):
@@ -198,30 +198,29 @@
             sums_now.append(total(acc))
         return tuple(sums_now)
 
-    def three(state, block, carry, reverse):
+    def three(state, at, step, carry, reverse, scaled):
         order = (2, 1, 0) if reverse else (0, 1, 2)
-        step = block - 5 * lax.shift_right_logical(block * 13108, 16)
-        at = lax.shift_right_logical(block * 13108, 16)
+        block = 5 * at + step
         row = home_of(at)
         tile_words = [words[3 * block + j] for j in order]
         if reverse:
-            last = step == 4
-            after = jnp.where(last, home_of(jnp.minimum(at + 1, GROUPS - 1)), row)
-            edge = beta[after, jnp.where(last, 0, 3 * step + 3)]
-            edge = jnp.where(block == BLOCKS - 1, 0.0, edge)
+            if step == 4:
+                edge = beta[home_of(jnp.minimum(at + 1, GROUPS - 1)), 0]
+                edge = jnp.where(at == GROUPS - 1, 0.0, edge)
+            else:
+                edge = beta[row, 3 * step + 3]
             rates = [edge, beta[row, 3 * step + 2], beta[row, 3 * step + 1]]
         else:
             rates = [beta[row, 3 * step + j] for j in range(3)]
         singles = order
         pairs = (4, 3) if reverse else (3, 4)
         result = [None] * TGT
-        new_scale = [jnp.ones((8, LANES), jnp.float32)] * TGT
         sums_of = {}
         emis = {t: [emission(row, 3 * step + j, t) for j in order] for t in range(TGT)}
 
         def down(targets):
             accs = {t: [None] * 3 for t in targets}
-            first = {t: (emis[t][0][0] * carry[4 + t], emis[t][0][1] * carry[4 + t]) for t in targets}
+            first = {t: tuple(e * carry[4 + t] for e in emis[t][0]) if scaled else emis[t][0] for t in targets}
             for v in range(TILES):
                 masks = [(w & (1 << (2 * v))) != 0 for w in tile_words]
                 for t in targets:
@@ -242,7 +241,7 @@
             for t in targets:
                 q1, q2, q3 = sums_of[t]
                 g = lambda q: gs[TGT * q + t, block]
-                m0 = rates[0] * (carry[t] * carry[4 + t])
+                m0 = rates[0] * (carry[t] * carry[4 + t] if scaled else carry[t])
                 s1 = q1 + m0 * g(singles[0])
                 m1 = rates[1] * s1
                 s2 = (q2 + m0 * g(pairs[0])) + m1 * g(singles[1])
@@ -262,18 +261,18 @@
         down((2, 3))
         up((0, 1))
         up((2, 3))
-        return tuple(result) + tuple(new_scale)
+        return tuple(result)
 
     start_sums, end_sums = sum_of(fwd), sum_of(bwd)
     copy.wait()
 
     def run(state, first, count_groups, reverse, sums_now):
         def one_group(i, sums_now):
-            block = (first - i if reverse else first + i) * 5
+            at = first - i if reverse else first + i
             carry = tuple(sums_now) + tuple(lift / s for s in sums_now)
-            def one_block(j, carry):
-                return three(state, block + (4 - j if reverse else j), carry, reverse)
-            return lax.fori_loop(0, 5, one_block, carry, unroll=5)[:TGT]
+            for j in range(5):
+                carry = three(state, at, 4 - j if reverse else j, carry, reverse, j == 0)
+            return carry
         return lax.fori_loop(0, count_groups, one_group, sums_now)
 
     fsum = run(fwd, 0, group, False, start_sums)

time: 69.2 us -> 69 us (level)
  no operation moved by 1% of the time
where the time goes in v4:
time: 69 us; the launch traced here: 68.6 us
  Pallas kernels  26.2 us (38%)
  starting transfers between devices  19.9 us (29%)
  blocking collectives  17.5 us (25%)
  waiting for transfers between devices  3.03 us (4%)
  other arithmetic  1.12 us (2%)
  local copies, waits for them, and re-layouts  0.84 us (1%)
    pallas_call x1, Pallas kernels, chains(): pl.pallas_call(kernel, out_shape=jax.ShapeDtypeStruct((TGT, SPAN), f32),...  22.5 us
    all_to_all x1, blocking collectives, local(): line = lax.all_to_all(message, 'z', 0, 0, tiled=True)  17.5 us
    all_to_all x1, starting transfers between devices, local(): lax.all_to_all(spread, ('x', 'y'), 0, 0, tiled=True).reshape(512, LANES)  9.67 us
    ppermute x1, starting transfers between devices, local(): other = lax.ppermute(own, 'c', swap)  5.96 us
    ppermute x1, starting transfers between devices, local(): partner = lax.ppermute(side, 'c', swap)  4.28 us
    pallas_call x1, Pallas kernels, planes(): pl.pallas_call(planes_kernel, out_shape=(laid, laid), in_specs=[vmem] * 2...  2.3 us
    all_to_all x1, waiting for transfers between devices, local(): lax.all_to_all(spread, ('x', 'y'), 0, 0, tiled=True).reshape(512, LANES)  1.95 us
    pallas_call x1, Pallas kernels, pack(): pl.pallas_call(pack_kernel, out_shape=jax.ShapeDtypeStruct((24, LANES), j...  1.4 us
  transfers between devices with their start and end apart: 3, of which 2 were waited for; matrix products, arithmetic and copies ran while one was open for 2% of the time, Pallas kernels for 3%

profile of v4, /device:TPU:1, one launch (start us, length us, event | category | flops | bytes accessed | tf_op | source)
XLA Modules:
  0.0 68.6 jit_solution(10563301724128556993)
XLA Ops:
  0.0 1.4 %shard_map.55 = s32[24,128]{1,0:T(8,128)} custom-call(s32[15,16]{1,0:T(8,128)} %alleles.1, s32[4,15]{1,0:T(4,128)} %bitcast.16, s32[1,15]{1,0:T(1,128)} %bitcast.17), custom_call_target="tpu_custom_call" | custom-call | tf_op jit(solution)/shard_map/pallas_call | solution.py:57
  1.4 17.5 %all_to_all.10 = s32[8,1,384]{2,1,0:T(1,128)S(1)} all-to-all(s32[8,1,384]{2,1,0:T(1,128)} %bitcast.12), channel_id=1, replica_groups=mesh['z'=8,'c'=2,'x'=4,'y'=8] {'z'}, dimensions={0} | all-to-all | bytes 24576 | tf_op jit(solution)/shard_map/all_to_all | solution.py:395
  18.9 0.8 %broadcast_in_dim.23 = s32[32,1,2048]{2,1,0:T(1,128)} broadcast(s32[2048]{0:T(1024)S(1)} %bitcast.13), dimensions={2} | broadcast | bytes 270336 | tf_op jit(solution)/shard_map/broadcast_in_dim | solution.py:396
  19.7 9.7 %all-to-all-start.1 = ((s32[32,1,2048]{2,1,0:T(1,128)}), s32[32,1,2048]{2,1,0:T(1,128)S(1)}, u32[]{:S(2)}, u32[]{:S(2)}) async-start(s32[32,1,2048]{2,1,0:T(1,128)} %broadcast_in_dim.23), calls=%async_computation.1 | async-start | bytes 524288 | tf_op jit(solution)/shard_map/all_to_all | solution.py:397
  29.4 2.3 %shard_map.56 = (f32[4,15,8,128]{3,2,1,0:T(8,128)}, f32[4,15,8,128]{3,2,1,0:T(8,128)}) custom-call(f32[4,15360]{1,0:T(4,128)} %weights_start.1, f32[4,15360]{1,0:T(4,128)} %weights_end.1), custom_call_target="tpu_custom_call" | custom-call | flops 4000000 | bytes 1000000 | tf_op jit(solution)/shard_map/pallas_call | solution.py:92
  31.7 4.3 %collective-permute-start = (s32[8,128]{1,0:T(8,128)S(1)}, s32[8,128]{1,0:T(8,128)S(1)}, u32[]{:S(2)}, u32[]{:S(2)}) collective-permute-start(s32[8,128]{1,0:T(8,128)S(1)} %bitcast.14), channel_id=1, source_target_pairs={{0,32},{32,0},{1,33},{33,1},{2,34},{34,2},{3,35},{35,3},{4,36},{36... | collective-permute-start | bytes 12296 | tf_op jit(solution)/shard_map/ppermute | solution.py:401
  36.0 1.1 %broadcast_maximum_fusion = (f32[4,15,8,128]{3,2,1,0:T(8,128)S(1)}, f32[4,15,8,128]{3,2,1,0:T(8,128)S(1)}) fusion(f32[4,15,8,128]{3,2,1,0:T(8,128)} %get-tuple-element.8, f32[4,15,8,128]{3,2,1,0:T(8,128)} %get-tuple-element.7), kind=kLoop, calls=%fused_computation | loop fusion | flops 122880 | bytes 983040 | tf_op jit(solution)/shard_map/max | solution.py:394
  37.1 1.9 %all-to-all-done.1 = s32[32,1,2048]{2,1,0:T(1,128)S(1)} async-done(((s32[32,1,2048]{2,1,0:T(1,128)}), s32[32,1,2048]{2,1,0:T(1,128)S(1)}, u32[]{:S(2)}, u32[]{:S(2)}) %all-to-all-start.1) | async-done | bytes 262176 | tf_op jit(solution)/shard_map/all_to_all | solution.py:397
  39.0 6.0 %collective-permute-start.1 = (s32[512,128]{1,0:T(8,128)S(1)}, s32[512,128]{1,0:T(8,128)S(1)}, u32[]{:S(2)}, u32[]{:S(2)}) collective-permute-start(s32[512,128]{1,0:T(8,128)S(1)} %bitcast.10), channel_id=1, source_target_pairs={{0,32},{32,0},{1,33},{33,1},{2,34},{34,2},{3,35},{35,3},{4,36},{36... | collective-permute-start | bytes 786440 | tf_op jit(solution)/shard_map/ppermute | solution.py:400
  45.0 0.0 collective-permute-done
  45.1 1.1 %collective-permute-done.1.other = s32[512,128]{1,0:T(8,128)S(1)} collective-permute-done((s32[512,128]{1,0:T(8,128)S(1)}, s32[512,128]{1,0:T(8,128)S(1)}, u32[]{:S(2)}, u32[]{:S(2)}) %collective-permute-start.1) | collective-permute-done | bytes 262176 | tf_op jit(solution)/shard_map/ppermute | solution.py:400
  46.1 22.5 %shard_map.57 = f32[4,15]{1,0:T(4,128)} custom-call(s32[1]{0:T(128)} %bitcast.place, f32[16,128]{1,0:T(8,128)S(1)} %get-tuple-element.10.beta, f32[16,128]{1,0:T(8,128)S(1)} %get-tuple-element.11.keep, f32[16,128]{1,0:T(8,128)S(1)} %get-tuple-element.12.for_one, f32[16,128]{1,0:T(8,128)S(1)} %get-tuple-element.9.for_zero, s32[16,128]{1,0:T(8,128)S(1)} %pad_add_fusion.sides, ...), custom_call_target="tpu_custom_call" | custom-call | tf_op jit(solution)/shard_map/pallas_call | solution.py:368
  (5 shorter events, 0.0 us)
Async XLA Ops:
  19.7 19.3 %all-to-all-start.1 = ((s32[32,1,2048]{2,1,0:T(1,128)}), s32[32,1,2048]{2,1,0:T(1,128)S(1)}, u32[]{:S(2)}, u32[]{:S(2)}) async-start(s32[32,1,2048]{2,1,0:T(1,128)} %broadcast_in_dim.23), calls=%async_computation.1 | async-start | bytes 524288 | tf_op jit(solution)/shard_map/all_to_all | solution.py:397
  31.7 13.3 %collective-permute-start = (s32[8,128]{1,0:T(8,128)S(1)}, s32[8,128]{1,0:T(8,128)S(1)}, u32[]{:S(2)}, u32[]{:S(2)}) collective-permute-start(s32[8,128]{1,0:T(8,128)S(1)} %bitcast.14), channel_id=1, source_target_pairs={{0,32},{32,0},{1,33},{33,1},{2,34},{34,2},{3,35},{35,3},{4,36},{36... | collective-permute-start | bytes 12296 | tf_op jit(solution)/shard_map/ppermute | solution.py:401
  39.0 7.1 %collective-permute-start.1 = (s32[512,128]{1,0:T(8,128)S(1)}, s32[512,128]{1,0:T(8,128)S(1)}, u32[]{:S(2)}, u32[]{:S(2)}) collective-permute-start(s32[512,128]{1,0:T(8,128)S(1)} %bitcast.10), channel_id=1, source_target_pairs={{0,32},{32,0},{1,33},{33,1},{2,34},{34,2},{3,35},{35,3},{4,36},{36... | collective-permute-start | bytes 786440 | tf_op jit(solution)/shard_map/ppermute | solution.py:400

commit v5 on v4

--- a/solution.py
+++ b/solution.py
@@ -146,7 +146,7 @@
                 words[first + m] = lax.shift_right_logical(picked, odd)
         return carry
 
-    lax.fori_loop(0, 8, unpack, 0, unroll=2)
+    lax.fori_loop(0, 8, unpack, 0)
 
     def emission(row, m, t):
         at = 16 + 15 * t + m

time: 69 us -> 70.2 us (1.017)
  Pallas kernels: 26.2 us -> 27.4 us
    pallas_call x1, Pallas kernels: 22.5 us -> 23.7 us  [chains(): pl.pallas_call(kernel, out_shape=jax.ShapeDtypeStruct((TGT, SPAN), f32),...]
where the time goes in v5:
time: 70.2 us; the launch traced here: 69.8 us
  Pallas kernels  27.4 us (39%)
  starting transfers between devices  19.9 us (28%)
  blocking collectives  17.5 us (25%)
  waiting for transfers between devices  3.03 us (4%)
  other arithmetic  1.12 us (2%)
  local copies, waits for them, and re-layouts  0.84 us (1%)
    pallas_call x1, Pallas kernels, chains(): pl.pallas_call(kernel, out_shape=jax.ShapeDtypeStruct((TGT, SPAN), f32),...  23.7 us
    all_to_all x1, blocking collectives, local(): line = lax.all_to_all(message, 'z', 0, 0, tiled=True)  17.5 us
    all_to_all x1, starting transfers between devices, local(): lax.all_to_all(spread, ('x', 'y'), 0, 0, tiled=True).reshape(512, LANES)  9.67 us
    ppermute x1, starting transfers between devices, local(): other = lax.ppermute(own, 'c', swap)  5.96 us
    ppermute x1, starting transfers between devices, local(): partner = lax.ppermute(side, 'c', swap)  4.28 us
    pallas_call x1, Pallas kernels, planes(): pl.pallas_call(planes_kernel, out_shape=(laid, laid), in_specs=[vmem] * 2...  2.3 us
    all_to_all x1, waiting for transfers between devices, local(): lax.all_to_all(spread, ('x', 'y'), 0, 0, tiled=True).reshape(512, LANES)  1.95 us
  transfers between devices with their start and end apart: 3, of which 2 were waited for; matrix products, arithmetic and copies ran while one was open for 2% of the time, Pallas kernels for 3%

profile of v5, /device:TPU:1, one launch (start us, length us, event | category | flops | bytes accessed | tf_op | source)
XLA Modules:
  0.0 69.8 jit_solution(16943608566408017577)
XLA Ops:
  0.0 1.4 %shard_map.55 = s32[24,128]{1,0:T(8,128)} custom-call(s32[15,16]{1,0:T(8,128)} %alleles.1, s32[4,15]{1,0:T(4,128)} %bitcast.16, s32[1,15]{1,0:T(1,128)} %bitcast.17), custom_call_target="tpu_custom_call" | custom-call | tf_op jit(solution)/shard_map/pallas_call | solution.py:57
  1.4 17.5 %all_to_all.10 = s32[8,1,384]{2,1,0:T(1,128)S(1)} all-to-all(s32[8,1,384]{2,1,0:T(1,128)} %bitcast.12), channel_id=1, replica_groups=mesh['z'=8,'c'=2,'x'=4,'y'=8] {'z'}, dimensions={0} | all-to-all | bytes 24576 | tf_op jit(solution)/shard_map/all_to_all | solution.py:395
  18.9 0.8 %broadcast_in_dim.23 = s32[32,1,2048]{2,1,0:T(1,128)} broadcast(s32[2048]{0:T(1024)S(1)} %bitcast.13), dimensions={2} | broadcast | bytes 270336 | tf_op jit(solution)/shard_map/broadcast_in_dim | solution.py:396
  19.7 9.7 %all-to-all-start.1 = ((s32[32,1,2048]{2,1,0:T(1,128)}), s32[32,1,2048]{2,1,0:T(1,128)S(1)}, u32[]{:S(2)}, u32[]{:S(2)}) async-start(s32[32,1,2048]{2,1,0:T(1,128)} %broadcast_in_dim.23), calls=%async_computation.1 | async-start | bytes 524288 | tf_op jit(solution)/shard_map/all_to_all | solution.py:397
  29.4 2.3 %shard_map.56 = (f32[4,15,8,128]{3,2,1,0:T(8,128)}, f32[4,15,8,128]{3,2,1,0:T(8,128)}) custom-call(f32[4,15360]{1,0:T(4,128)} %weights_start.1, f32[4,15360]{1,0:T(4,128)} %weights_end.1), custom_call_target="tpu_custom_call" | custom-call | flops 4000000 | bytes 1000000 | tf_op jit(solution)/shard_map/pallas_call | solution.py:92
  31.7 4.3 %collective-permute-start = (s32[8,128]{1,0:T(8,128)S(1)}, s32[8,128]{1,0:T(8,128)S(1)}, u32[]{:S(2)}, u32[]{:S(2)}) collective-permute-start(s32[8,128]{1,0:T(8,128)S(1)} %bitcast.14), channel_id=1, source_target_pairs={{0,32},{32,0},{1,33},{33,1},{2,34},{34,2},{3,35},{35,3},{4,36},{36... | collective-permute-start | bytes 12296 | tf_op jit(solution)/shard_map/ppermute | solution.py:401
  36.0 1.1 %broadcast_maximum_fusion = (f32[4,15,8,128]{3,2,1,0:T(8,128)S(1)}, f32[4,15,8,128]{3,2,1,0:T(8,128)S(1)}) fusion(f32[4,15,8,128]{3,2,1,0:T(8,128)} %get-tuple-element.8, f32[4,15,8,128]{3,2,1,0:T(8,128)} %get-tuple-element.7), kind=kLoop, calls=%fused_computation | loop fusion | flops 122880 | bytes 983040 | tf_op jit(solution)/shard_map/max | solution.py:394
  37.1 1.9 %all-to-all-done.1 = s32[32,1,2048]{2,1,0:T(1,128)S(1)} async-done(((s32[32,1,2048]{2,1,0:T(1,128)}), s32[32,1,2048]{2,1,0:T(1,128)S(1)}, u32[]{:S(2)}, u32[]{:S(2)}) %all-to-all-start.1) | async-done | bytes 262176 | tf_op jit(solution)/shard_map/all_to_all | solution.py:397
  39.0 6.0 %collective-permute-start.1 = (s32[512,128]{1,0:T(8,128)S(1)}, s32[512,128]{1,0:T(8,128)S(1)}, u32[]{:S(2)}, u32[]{:S(2)}) collective-permute-start(s32[512,128]{1,0:T(8,128)S(1)} %bitcast.10), channel_id=1, source_target_pairs={{0,32},{32,0},{1,33},{33,1},{2,34},{34,2},{3,35},{35,3},{4,36},{36... | collective-permute-start | bytes 786440 | tf_op jit(solution)/shard_map/ppermute | solution.py:400
  45.0 0.0 collective-permute-done
  45.1 1.1 %collective-permute-done.1.other = s32[512,128]{1,0:T(8,128)S(1)} collective-permute-done((s32[512,128]{1,0:T(8,128)S(1)}, s32[512,128]{1,0:T(8,128)S(1)}, u32[]{:S(2)}, u32[]{:S(2)}) %collective-permute-start.1) | collective-permute-done | bytes 262176 | tf_op jit(solution)/shard_map/ppermute | solution.py:400
  46.1 23.7 %shard_map.57 = f32[4,15]{1,0:T(4,128)} custom-call(s32[1]{0:T(128)} %bitcast.place, f32[16,128]{1,0:T(8,128)S(1)} %get-tuple-element.10.beta, f32[16,128]{1,0:T(8,128)S(1)} %get-tuple-element.11.keep, f32[16,128]{1,0:T(8,128)S(1)} %get-tuple-element.12.for_one, f32[16,128]{1,0:T(8,128)S(1)} %get-tuple-element.9.for_zero, s32[16,128]{1,0:T(8,128)S(1)} %pad_add_fusion.sides, ...), custom_call_target="tpu_custom_call" | custom-call | tf_op jit(solution)/shard_map/pallas_call | solution.py:368
  (5 shorter events, 0.0 us)
Async XLA Ops:
  19.7 19.3 %all-to-all-start.1 = ((s32[32,1,2048]{2,1,0:T(1,128)}), s32[32,1,2048]{2,1,0:T(1,128)S(1)}, u32[]{:S(2)}, u32[]{:S(2)}) async-start(s32[32,1,2048]{2,1,0:T(1,128)} %broadcast_in_dim.23), calls=%async_computation.1 | async-start | bytes 524288 | tf_op jit(solution)/shard_map/all_to_all | solution.py:397
  31.7 13.3 %collective-permute-start = (s32[8,128]{1,0:T(8,128)S(1)}, s32[8,128]{1,0:T(8,128)S(1)}, u32[]{:S(2)}, u32[]{:S(2)}) collective-permute-start(s32[8,128]{1,0:T(8,128)S(1)} %bitcast.14), channel_id=1, source_target_pairs={{0,32},{32,0},{1,33},{33,1},{2,34},{34,2},{3,35},{35,3},{4,36},{36... | collective-permute-start | bytes 12296 | tf_op jit(solution)/shard_map/ppermute | solution.py:401
  39.0 7.1 %collective-permute-start.1 = (s32[512,128]{1,0:T(8,128)S(1)}, s32[512,128]{1,0:T(8,128)S(1)}, u32[]{:S(2)}, u32[]{:S(2)}) collective-permute-start(s32[512,128]{1,0:T(8,128)S(1)} %bitcast.10), channel_id=1, source_target_pairs={{0,32},{32,0},{1,33},{33,1},{2,34},{34,2},{3,35},{35,3},{4,36},{36... | collective-permute-start | bytes 786440 | tf_op jit(solution)/shard_map/ppermute | solution.py:400
